TPU v7x, 256 devices: a whole 4x4x8 slice. The times are simulated.
256 devices in a mesh: gx: 4 (over z_hi, core), gy: 4 (over z_lo), gz: 16 (over x, y).
Axes of the slice: x: 4, y: 4, z: 8 (z_hi: 2, z_lo: 4; z = z_hi * 4 + z_lo), core: 2. Of those that a mesh axis runs over, the one named last changes fastest.
Arguments:
- charges: float32 [512, 128, 512], P('gz', 'gy', 'gx'), may hold values from -8 to 8
- kernel_taps: float32 [3, 2, 17], replicated, may hold values from 0 to 2
Outputs:
- potential: float32 [512, 128, 512], P('gz', 'gy', 'gx')
All inputs are finite; a program needn't handle non-finite values.
Results may differ from a plain program's by a relative error of at most 0.0001.
Values sent between devices are 32-bit elements; how exact they have to be, the bound alone decides.
A program may use at most 128 MiB of HBM per device.

v0:
```python
import jax
import jax.numpy as jnp
from jax import lax
from jax.sharding import PartitionSpec as P

RADIUS = 8
TAPS = 17


RESTRICT_WEIGHTS = ((-3, -0.0625), (-1, 0.5625), (0, 1.0), (1, 0.5625), (3, -0.0625))


def extended(x, sides, width):
    for axis, dim in sides:
        count, length = (lax.axis_size(axis), x.shape[dim])
        up = [(i, (i + 1) % count) for i in range(count - 1)]
        down = [(j, i) for i, j in up]
        last = lax.slice_in_dim(x, length - width, length, axis=dim)
        initial = lax.slice_in_dim(x, 0, width, axis=dim)
        before = lax.ppermute(last, axis, up)
        after = lax.ppermute(initial, axis, down)
        x = jnp.concatenate([before, x, after], axis=dim)
    return x


def convolve_axis(padded, kernel_rows, axis_dim, length):
    weight_shape = (kernel_rows.shape[0],) + (1,) * (padded.ndim - 1)
    summed = kernel_rows[:, 0].reshape(weight_shape) * lax.slice_in_dim(
        padded, 0, length, axis=axis_dim
    )
    for offset in range(1, TAPS):
        summed = summed + kernel_rows[:, offset].reshape(weight_shape) * lax.slice_in_dim(
            padded, offset, offset + length, axis=axis_dim
        )
    return summed


def stencil_box(padded, kernel_rows, extent_z, extent_y, extent_x):
    smoothed = convolve_axis(padded[None], kernel_rows, 1, extent_z)
    smoothed = convolve_axis(smoothed, kernel_rows, 2, extent_y)
    smoothed = convolve_axis(smoothed, kernel_rows, 3, extent_x)
    return jnp.sum(smoothed, axis=0)


def restrict_axis(padded, axis_dim, margin, count):
    summed = None
    for offset, weight in RESTRICT_WEIGHTS:
        first = margin + offset
        piece = lax.slice_in_dim(padded, first, first + 2 * count - 1, stride=2, axis=axis_dim)
        summed = weight * piece if summed is None else summed + weight * piece
    return summed


def restrict_padded(padded, margin, counts):
    result_field = restrict_axis(padded, 0, margin, counts[0])
    result_field = restrict_axis(result_field, 1, margin, counts[1])
    return restrict_axis(result_field, 2, margin, counts[2])


def prolong_axis(padded, axis_dim, margin, count):

    def take(shift):
        return lax.slice_in_dim(padded, margin + shift, margin + shift + count, axis=axis_dim)

    centre = take(0)
    odd_cells = 0.5625 * (centre + take(1)) - 0.0625 * (take(-1) + take(2))
    stacked = jnp.stack([centre, odd_cells], axis=axis_dim + 1)
    new_shape = list(centre.shape)
    new_shape[axis_dim] = 2 * count
    return stacked.reshape(new_shape)


def prolong_padded(padded, margin, counts):
    result_field = prolong_axis(padded, 0, margin, counts[0])
    result_field = prolong_axis(result_field, 1, margin, counts[1])
    return prolong_axis(result_field, 2, margin, counts[2])


def local(charges, kernel_taps):
    extent_z, extent_y, extent_x = charges.shape
    along_z = extended(charges, (("gz", 0),), RADIUS)
    along_y = extended(along_z, (("gy", 1),), RADIUS)
    fine_padded = extended(along_y, (("gx", 2),), RADIUS)
    fine_potential = stencil_box(fine_padded, kernel_taps[0], extent_z, extent_y, extent_x)
    mid_z, mid_y, mid_x = (extent_z // 2, extent_y // 2, extent_x // 2)
    mid_charges = restrict_padded(fine_padded, RADIUS, (mid_z, mid_y, mid_x))
    mid_padded = extended(mid_charges, (("gx", 2), ("gy", 1), ("gz", 0)), RADIUS)
    mid_potential = stencil_box(mid_padded, kernel_taps[1], mid_z, mid_y, mid_x)
    coarse_z, coarse_y, coarse_x = (mid_z // 2, mid_y // 2, mid_x // 2)
    coarse_charges = restrict_padded(mid_padded, RADIUS, (coarse_z, coarse_y, coarse_x))
    coarse_padded = extended(coarse_charges, (("gx", 2), ("gy", 1), ("gz", 0)), RADIUS)
    coarse_potential = stencil_box(coarse_padded, kernel_taps[2], coarse_z, coarse_y, coarse_x)
    coarse_wide = extended(coarse_potential, (("gx", 2), ("gy", 1), ("gz", 0)), 2)
    mid_total = mid_potential + prolong_padded(coarse_wide, 2, (coarse_z, coarse_y, coarse_x))
    mid_wide = extended(mid_total, (("gx", 2), ("gy", 1), ("gz", 0)), 2)
    return fine_potential + prolong_padded(mid_wide, 2, (mid_z, mid_y, mid_x))


def solution(mesh):
    return jax.shard_map(
        local,
        mesh=mesh,
        in_specs=(P("gz", "gy", "gx"), P()),
        out_specs=P("gz", "gy", "gx"),
        check_vma=False,
    )
```

profile of v0, /device:TPU:7, one launch (start us, length us, event | category | flops | bytes accessed | tf_op | source)
XLA Modules:
  0.0 222.4 jit_solution(1430556707831646082)
XLA Ops:
  4.2 4.2 %collective-permute-start.1 = (f32[8,32,128]{2,1,0:T(8,128)S(1)}, f32[8,32,128]{2,1,0:T(8,128)S(1)}, u32[]{:S(2)}, u32[]{:S(2)}) collective-permute-start(f32[8,32,128]{2,1,0:T(8,128)S(1)} %get-tuple-element.96), channel_id=1, source_target_pairs={{1,0},{2,1},{3,2},{4,3},{5,4},{6,5},{7,6},{8,7},{9,8},{10,9},{11,1... | collective-permute-start | bytes 393224 | tf_op jit(solution)/shard_map/ppermute | solution.py:21
  10.6 3.6 %collective-permute-start.2 = (f32[48,8,128]{2,1,0:T(8,128)S(1)}, f32[48,8,128]{2,1,0:T(8,128)S(1)}, u32[]{:S(2)}, u32[]{:S(2)}) collective-permute-start(f32[48,8,128]{2,1,0:T(8,128)S(1)} %get-tuple-element.75), channel_id=1, source_target_pairs={{0,16},{16,32},{32,48},{1,17},{17,33},{33,49},{2,18},{18,34},{34,5... | collective-permute-start | bytes 589832 | tf_op jit(solution)/shard_map/ppermute | solution.py:20
  16.7 4.0 %collective-permute-done.3 = f32[48,8,128]{2,1,0:T(8,128)S(1)} collective-permute-done((f32[48,8,128]{2,1,0:T(8,128)S(1)}, f32[48,8,128]{2,1,0:T(8,128)S(1)}, u32[]{:S(2)}, u32[]{:S(2)}) %collective-permute-start.3) | collective-permute-done | bytes 196640 | tf_op jit(solution)/shard_map/ppermute | solution.py:21
  22.5 4.8 %collective-permute-start.5 = (f32[48,48,8]{1,2,0:T(8,128)S(1)}, f32[48,48,8]{1,2,0:T(8,128)}, u32[]{:S(2)}, u32[]{:S(2)}) collective-permute-start(f32[48,48,8]{1,2,0:T(8,128)S(1)} %copy.215), channel_id=1, source_target_pairs={{64,0},{128,64},{192,128},{65,1},{129,65},{193,129},{66,2},{130,66... | collective-permute-start | bytes 221192 | tf_op jit(solution)/shard_map/ppermute | solution.py:21
  27.4 7.8 %collective-permute-start.4 = (f32[48,48,8]{1,2,0:T(8,128)}, f32[48,48,8]{1,2,0:T(8,128)S(1)}, u32[]{:S(2)}, u32[]{:S(2)}) collective-permute-start(f32[48,48,8]{1,2,0:T(8,128)} %copy.214), channel_id=1, source_target_pairs={{0,64},{64,128},{128,192},{1,65},{65,129},{129,193},{2,66},{66,130... | collective-permute-start | bytes 221192 | tf_op jit(solution)/shard_map/ppermute | solution.py:20
  56.2 8.3 %collective-permute-start.6 = (f32[16,16,8]{2,1,0:T(8,128)S(1)}, f32[16,16,8]{2,1,0:T(8,128)S(1)}, u32[]{:S(2)}, u32[]{:S(2)}) collective-permute-start(f32[16,16,8]{2,1,0:T(8,128)S(1)} %get-tuple-element.129), channel_id=1, source_target_pairs={{0,64},{64,128},{128,192},{1,65},{65,129},{129,193},{2,66},{66,130... | collective-permute-start | bytes 24584 | tf_op jit(solution)/shard_map/ppermute | solution.py:20
  67.4 7.3 %collective-permute-done.7 = f32[16,16,8]{2,1,0:T(8,128)S(1)} collective-permute-done((f32[16,16,8]{2,1,0:T(8,128)S(1)}, f32[16,16,8]{2,1,0:T(8,128)S(1)}, u32[]{:S(2)}, u32[]{:S(2)}) %collective-permute-start.7) | collective-permute-done | bytes 8224 | tf_op jit(solution)/shard_map/ppermute | solution.py:21
  74.9 5.1 %collective-permute-start.8 = (f32[16,8,80]{2,1,0:T(8,128)S(1)}, f32[16,8,80]{2,1,0:T(8,128)S(1)}, u32[]{:S(2)}, u32[]{:S(2)}) collective-permute-start(f32[16,8,80]{2,1,0:T(8,128)S(1)} %get-tuple-element.127), channel_id=1, source_target_pairs={{0,16},{16,32},{32,48},{1,17},{17,33},{33,49},{2,18},{18,34},{34,5... | collective-permute-start | bytes 122888 | tf_op jit(solution)/shard_map/ppermute | solution.py:20
  88.3 5.2 %collective-permute-start.11 = (f32[8,32,80]{2,1,0:T(8,128)S(1)}, f32[8,32,80]{2,1,0:T(8,128)S(1)}, u32[]{:S(2)}, u32[]{:S(2)}) collective-permute-start(f32[8,32,80]{2,1,0:T(8,128)S(1)} %get-tuple-element.120), channel_id=1, source_target_pairs={{1,0},{2,1},{3,2},{4,3},{5,4},{6,5},{7,6},{8,7},{9,8},{10,9},{11,1... | collective-permute-start | bytes 245768 | tf_op jit(solution)/shard_map/ppermute | solution.py:21
  98.8 3.4 %collective-permute-start.12 = (f32[8,8,8]{2,1,0:T(8,128)S(1)}, f32[8,8,8]{2,1,0:T(8,128)S(1)}, u32[]{:S(2)}, u32[]{:S(2)}) collective-permute-start(f32[8,8,8]{2,1,0:T(8,128)S(1)} %get-tuple-element.141), channel_id=1, source_target_pairs={{0,64},{64,128},{128,192},{1,65},{65,129},{129,193},{2,66},{66,130... | collective-permute-start | bytes 6152 | tf_op jit(solution)/shard_map/ppermute | solution.py:20
  104.4 8.9 %slice_bitcast_fusion.16 = (f32[32,48,144]{2,1,0:T(8,128)}, f32[32,48,144]{2,1,0:T(8,128)}, f32[32,48,144]{2,1,0:T(8,128)}, f32[32,48,144]{2,1,0:T(8,128)}, f32[...) fusion(f32[1,48,48,144]{3,2,1,0:T(8,128)S(1)} %fusion.136), kind=kLoop, calls=%fused_computation.51 | loop fusion | bytes 30081024 | tf_op jit(solution)/shard_map/mul | solution.py:28
  114.7 4.0 %collective-permute-start.14 = (f32[8,8,48]{2,1,0:T(8,128)S(1)}, f32[8,8,48]{2,1,0:T(8,128)S(1)}, u32[]{:S(2)}, u32[]{:S(2)}) collective-permute-start(f32[8,8,48]{2,1,0:T(8,128)S(1)} %pad_maximum_fusion.26), channel_id=1, source_target_pairs={{0,16},{16,32},{32,48},{1,17},{17,33},{33,49},{2,18},{18,34},{34,5... | collective-permute-start | bytes 36872 | tf_op jit(solution)/shard_map/ppermute | solution.py:20
  119.8 5.9 %collective-permute-start.17 = (f32[8,24,48]{2,1,0:T(8,128)S(1)}, f32[8,24,48]{2,1,0:T(8,128)S(1)}, u32[]{:S(2)}, u32[]{:S(2)}) collective-permute-start(f32[8,24,48]{2,1,0:T(8,128)S(1)} %pad_maximum_fusion.18), channel_id=1, source_target_pairs={{1,0},{2,1},{3,2},{4,3},{5,4},{6,5},{7,6},{8,7},{9,8},{10,9},{11,1... | collective-permute-start | bytes 110600 | tf_op jit(solution)/shard_map/ppermute | solution.py:21
  128.4 5.2 %collective-permute-done.16 = f32[8,24,48]{2,1,0:T(8,128)S(1)} collective-permute-done((f32[8,24,48]{2,1,0:T(8,128)S(1)}, f32[8,24,48]{2,1,0:T(8,128)S(1)}, u32[]{:S(2)}, u32[]{:S(2)}) %collective-permute-start.16) | collective-permute-done | bytes 36896 | tf_op jit(solution)/shard_map/ppermute | solution.py:20
  135.0 9.7 %collective-permute-start.18 = (f32[8,8,2]{2,1,0:T(8,128)S(1)}, f32[8,8,2]{2,1,0:T(8,128)S(1)}, u32[]{:S(2)}, u32[]{:S(2)}) collective-permute-start(f32[8,8,2]{2,1,0:T(8,128)S(1)} %get-tuple-element.139), channel_id=1, source_target_pairs={{0,64},{64,128},{128,192},{1,65},{65,129},{129,193},{2,66},{66,130... | collective-permute-start | bytes 1544 | tf_op jit(solution)/shard_map/ppermute | solution.py:20
  147.5 6.4 %collective-permute-done.19 = f32[8,8,2]{2,1,0:T(8,128)S(1)} collective-permute-done((f32[8,8,2]{2,1,0:T(8,128)S(1)}, f32[8,8,2]{2,1,0:T(8,128)S(1)}, u32[]{:S(2)}, u32[]{:S(2)}) %collective-permute-start.19) | collective-permute-done | bytes 544 | tf_op jit(solution)/shard_map/ppermute | solution.py:21
  154.0 3.9 %collective-permute-start.20 = (f32[8,2,36]{2,1,0:T(2,128)S(1)}, f32[8,2,36]{2,1,0:T(2,128)S(1)}, u32[]{:S(2)}, u32[]{:S(2)}) collective-permute-start(f32[8,2,36]{2,1,0:T(2,128)S(1)} %get-tuple-element.135), channel_id=1, source_target_pairs={{0,16},{16,32},{32,48},{1,17},{17,33},{33,49},{2,18},{18,34},{34,5... | collective-permute-start | bytes 6920 | tf_op jit(solution)/shard_map/ppermute | solution.py:20
  165.6 3.4 %collective-permute-start.23 = (f32[2,12,36]{2,1,0:T(8,128)S(1)}, f32[2,12,36]{2,1,0:T(8,128)S(1)}, u32[]{:S(2)}, u32[]{:S(2)}) collective-permute-start(f32[2,12,36]{2,1,0:T(8,128)S(1)} %get-tuple-element.137), channel_id=1, source_target_pairs={{0,1},{1,2},{2,3},{3,4},{4,5},{5,6},{6,7},{7,8},{8,9},{9,10},{10,1... | collective-permute-start | bytes 10376 | tf_op jit(solution)/shard_map/ppermute | solution.py:20
  175.4 4.5 %collective-permute-start.24 = (f32[16,16,2]{2,1,0:T(8,128)S(1)}, f32[16,16,2]{2,1,0:T(8,128)S(1)}, u32[]{:S(2)}, u32[]{:S(2)}) collective-permute-start(f32[16,16,2]{2,1,0:T(8,128)S(1)} %get-tuple-element.123), channel_id=1, source_target_pairs={{0,64},{64,128},{128,192},{1,65},{65,129},{129,193},{2,66},{66,130... | collective-permute-start | bytes 6152 | tf_op jit(solution)/shard_map/ppermute | solution.py:20
  182.0 10.8 %multiply_add_fusion = f32[2,32,48,144]{3,2,1,0:T(8,128)S(1)} fusion(f32[32,48,144]{2,1,0:T(8,128)S(1)} %copy-done.5, f32[2]{0:T(128)S(1)} %copy-done.53, f32[32,48,144]{2,1,0:T(8,128)} %get-tuple-element.58, f32[2]{0:T(128)S(1)} %copy-done.54, f32[32,48,144]{2,1,0:T(8,128)} %get-tuple-element.59, f32[2]{0:T(128)S(1)} %copy-done.55, ...), kind=kLoop, calls=%fused_computation | loop fusion | flops 14598144 | bytes 16810120 | tf_op jit(solution)/shard_map/add | solution.py:32
  194.3 4.2 %collective-permute-start.26 = (f32[16,2,68]{2,0,1:T(8,128)S(1)}, f32[16,2,68]{2,0,1:T(8,128)S(1)}, u32[]{:S(2)}, u32[]{:S(2)}) collective-permute-start(f32[16,2,68]{2,0,1:T(8,128)S(1)} %copy.202), channel_id=1, source_target_pairs={{0,16},{16,32},{32,48},{1,17},{17,33},{33,49},{2,18},{18,34},{34,5... | collective-permute-start | bytes 26120 | tf_op jit(solution)/shard_map/ppermute | solution.py:20
  198.7 4.3 %fusion = f32[2,32,32,144]{3,2,1,0:T(8,128)S(1)} fusion(f32[2,32,48,144]{3,2,1,0:T(8,128)S(1)} %multiply_add_fusion, f32[2]{0:T(128)S(1)} %copy-done.53, f32[2]{0:T(128)S(1)} %copy-done.54, f32[2]{0:T(128)S(1)} %copy-done.55, f32[2]{0:T(128)S(1)} %copy-done.56, f32[2]{0:T(128)S(1)} %copy-done.57, f32[2]{0:T(128)S(1)} %copy-done.58, f32[2]{0:T(128)S(1)} %copy-done.59, ...), kind=kLoop, calls=%fused_computation.3 | loop fusion | flops 9732096 | bytes 21233800 | tf_op jit(solution)/shard_map/add | solution.py:32
  205.2 5.3 %fusion.17 = f32[32,32,128]{2,1,0:T(8,128)} fusion(f32[2,32,32,144]{3,2,1,0:T(8,128)S(1)} %fusion, f32[2]{0:T(128)S(1)} %copy-done.53, f32[2]{0:T(128)S(1)} %copy-done.54, f32[2]{0:T(128)S(1)} %copy-done.55, f32[2]{0:T(128)S(1)} %copy-done.56, f32[2]{0:T(128)S(1)} %copy-done.57, f32[2]{0:T(128)S(1)} %copy-done.58, f32[2]{0:T(128)S(1)} %copy-done.59, ...), kind=kLoop, calls=%fused_computation.55 | loop fusion | flops 8781824 | bytes 18350216 | tf_op jit(solution)/shard_map/reduce_sum | solution.py:42
  210.5 3.4 %collective-permute-start.29 = (f32[2,20,68]{2,1,0:T(8,128)S(1)}, f32[2,20,68]{2,1,0:T(8,128)S(1)}, u32[]{:S(2)}, u32[]{:S(2)}) collective-permute-start(f32[2,20,68]{2,1,0:T(8,128)S(1)} %get-tuple-element.121), channel_id=1, source_target_pairs={{0,1},{1,2},{2,3},{3,4},{4,5},{5,6},{6,7},{7,8},{8,9},{9,10},{10,1... | collective-permute-start | bytes 32648 | tf_op jit(solution)/shard_map/ppermute | solution.py:20
  (278 shorter events, 86.9 us)
Async XLA Ops:
  1.0 8.4 %collective-permute-start = (f32[8,32,128]{2,1,0:T(8,128)S(1)}, f32[8,32,128]{2,1,0:T(8,128)S(1)}, u32[]{:S(2)}, u32[]{:S(2)}) collective-permute-start(f32[8,32,128]{2,1,0:T(8,128)S(1)} %get-tuple-element.97), channel_id=1, source_target_pairs={{0,1},{1,2},{2,3},{3,4},{4,5},{5,6},{6,7},{7,8},{8,9},{9,10},{10,1... | collective-permute-start | bytes 393224 | tf_op jit(solution)/shard_map/ppermute | solution.py:20
  4.2 6.3 %collective-permute-start.1 = (f32[8,32,128]{2,1,0:T(8,128)S(1)}, f32[8,32,128]{2,1,0:T(8,128)S(1)}, u32[]{:S(2)}, u32[]{:S(2)}) collective-permute-start(f32[8,32,128]{2,1,0:T(8,128)S(1)} %get-tuple-element.96), channel_id=1, source_target_pairs={{1,0},{2,1},{3,2},{4,3},{5,4},{6,5},{7,6},{8,7},{9,8},{10,9},{11,1... | collective-permute-start | bytes 393224 | tf_op jit(solution)/shard_map/ppermute | solution.py:21
  14.1 6.6 %collective-permute-start.3 = (f32[48,8,128]{2,1,0:T(8,128)S(1)}, f32[48,8,128]{2,1,0:T(8,128)S(1)}, u32[]{:S(2)}, u32[]{:S(2)}) collective-permute-start(f32[48,8,128]{2,1,0:T(8,128)S(1)} %get-tuple-element.76), channel_id=1, source_target_pairs={{16,0},{32,16},{48,32},{17,1},{33,17},{49,33},{18,2},{34,18},{50,3... | collective-permute-start | bytes 589832 | tf_op jit(solution)/shard_map/ppermute | solution.py:21
  22.5 17.1 %collective-permute-start.5 = (f32[48,48,8]{1,2,0:T(8,128)S(1)}, f32[48,48,8]{1,2,0:T(8,128)}, u32[]{:S(2)}, u32[]{:S(2)}) collective-permute-start(f32[48,48,8]{1,2,0:T(8,128)S(1)} %copy.215), channel_id=1, source_target_pairs={{64,0},{128,64},{192,128},{65,1},{129,65},{193,129},{66,2},{130,66... | collective-permute-start | bytes 221192 | tf_op jit(solution)/shard_map/ppermute | solution.py:21
  27.4 11.8 %collective-permute-start.4 = (f32[48,48,8]{1,2,0:T(8,128)}, f32[48,48,8]{1,2,0:T(8,128)S(1)}, u32[]{:S(2)}, u32[]{:S(2)}) collective-permute-start(f32[48,48,8]{1,2,0:T(8,128)} %copy.214), channel_id=1, source_target_pairs={{0,64},{64,128},{128,192},{1,65},{65,129},{129,193},{2,66},{66,130... | collective-permute-start | bytes 221192 | tf_op jit(solution)/shard_map/ppermute | solution.py:20
  56.2 11.2 %collective-permute-start.6 = (f32[16,16,8]{2,1,0:T(8,128)S(1)}, f32[16,16,8]{2,1,0:T(8,128)S(1)}, u32[]{:S(2)}, u32[]{:S(2)}) collective-permute-start(f32[16,16,8]{2,1,0:T(8,128)S(1)} %get-tuple-element.129), channel_id=1, source_target_pairs={{0,64},{64,128},{128,192},{1,65},{65,129},{129,193},{2,66},{66,130... | collective-permute-start | bytes 24584 | tf_op jit(solution)/shard_map/ppermute | solution.py:20
  64.5 10.2 %collective-permute-start.7 = (f32[16,16,8]{2,1,0:T(8,128)S(1)}, f32[16,16,8]{2,1,0:T(8,128)S(1)}, u32[]{:S(2)}, u32[]{:S(2)}) collective-permute-start(f32[16,16,8]{2,1,0:T(8,128)S(1)} %get-tuple-element.130), channel_id=1, source_target_pairs={{64,0},{128,64},{192,128},{65,1},{129,65},{193,129},{66,2},{130,66... | collective-permute-start | bytes 24584 | tf_op jit(solution)/shard_map/ppermute | solution.py:21
  74.9 7.5 %collective-permute-start.8 = (f32[16,8,80]{2,1,0:T(8,128)S(1)}, f32[16,8,80]{2,1,0:T(8,128)S(1)}, u32[]{:S(2)}, u32[]{:S(2)}) collective-permute-start(f32[16,8,80]{2,1,0:T(8,128)S(1)} %get-tuple-element.127), channel_id=1, source_target_pairs={{0,16},{16,32},{32,48},{1,17},{17,33},{33,49},{2,18},{18,34},{34,5... | collective-permute-start | bytes 122888 | tf_op jit(solution)/shard_map/ppermute | solution.py:20
  85.2 10.9 %collective-permute-start.10 = (f32[8,32,80]{2,1,0:T(8,128)S(1)}, f32[8,32,80]{2,1,0:T(8,128)S(1)}, u32[]{:S(2)}, u32[]{:S(2)}) collective-permute-start(f32[8,32,80]{2,1,0:T(8,128)S(1)} %get-tuple-element.119), channel_id=1, source_target_pairs={{0,1},{1,2},{2,3},{3,4},{4,5},{5,6},{6,7},{7,8},{8,9},{9,10},{10,1... | collective-permute-start | bytes 245768 | tf_op jit(solution)/shard_map/ppermute | solution.py:20
  88.3 7.8 %collective-permute-start.11 = (f32[8,32,80]{2,1,0:T(8,128)S(1)}, f32[8,32,80]{2,1,0:T(8,128)S(1)}, u32[]{:S(2)}, u32[]{:S(2)}) collective-permute-start(f32[8,32,80]{2,1,0:T(8,128)S(1)} %get-tuple-element.120), channel_id=1, source_target_pairs={{1,0},{2,1},{3,2},{4,3},{5,4},{6,5},{7,6},{8,7},{9,8},{10,9},{11,1... | collective-permute-start | bytes 245768 | tf_op jit(solution)/shard_map/ppermute | solution.py:21
  98.8 14.4 %collective-permute-start.12 = (f32[8,8,8]{2,1,0:T(8,128)S(1)}, f32[8,8,8]{2,1,0:T(8,128)S(1)}, u32[]{:S(2)}, u32[]{:S(2)}) collective-permute-start(f32[8,8,8]{2,1,0:T(8,128)S(1)} %get-tuple-element.141), channel_id=1, source_target_pairs={{0,64},{64,128},{128,192},{1,65},{65,129},{129,193},{2,66},{66,130... | collective-permute-start | bytes 6152 | tf_op jit(solution)/shard_map/ppermute | solution.py:20
  102.3 11.0 %collective-permute-start.13 = (f32[8,8,8]{2,1,0:T(8,128)S(1)}, f32[8,8,8]{2,1,0:T(8,128)S(1)}, u32[]{:S(2)}, u32[]{:S(2)}) collective-permute-start(f32[8,8,8]{2,1,0:T(8,128)S(1)} %get-tuple-element.142), channel_id=1, source_target_pairs={{64,0},{128,64},{192,128},{65,1},{129,65},{193,129},{66,2},{130,66... | collective-permute-start | bytes 6152 | tf_op jit(solution)/shard_map/ppermute | solution.py:21
  119.8 8.6 %collective-permute-start.17 = (f32[8,24,48]{2,1,0:T(8,128)S(1)}, f32[8,24,48]{2,1,0:T(8,128)S(1)}, u32[]{:S(2)}, u32[]{:S(2)}) collective-permute-start(f32[8,24,48]{2,1,0:T(8,128)S(1)} %pad_maximum_fusion.18), channel_id=1, source_target_pairs={{1,0},{2,1},{3,2},{4,3},{5,4},{6,5},{7,6},{8,7},{9,8},{10,9},{11,1... | collective-permute-start | bytes 110600 | tf_op jit(solution)/shard_map/ppermute | solution.py:21
  125.7 7.9 %collective-permute-start.16 = (f32[8,24,48]{2,1,0:T(8,128)S(1)}, f32[8,24,48]{2,1,0:T(8,128)S(1)}, u32[]{:S(2)}, u32[]{:S(2)}) collective-permute-start(f32[8,24,48]{2,1,0:T(8,128)S(1)} %pad_maximum_fusion.18), channel_id=1, source_target_pairs={{0,1},{1,2},{2,3},{3,4},{4,5},{5,6},{6,7},{7,8},{8,9},{9,10},{10,1... | collective-permute-start | bytes 110600 | tf_op jit(solution)/shard_map/ppermute | solution.py:20
  135.0 12.4 %collective-permute-start.18 = (f32[8,8,2]{2,1,0:T(8,128)S(1)}, f32[8,8,2]{2,1,0:T(8,128)S(1)}, u32[]{:S(2)}, u32[]{:S(2)}) collective-permute-start(f32[8,8,2]{2,1,0:T(8,128)S(1)} %get-tuple-element.139), channel_id=1, source_target_pairs={{0,64},{64,128},{128,192},{1,65},{65,129},{129,193},{2,66},{66,130... | collective-permute-start | bytes 1544 | tf_op jit(solution)/shard_map/ppermute | solution.py:20
  144.7 9.1 %collective-permute-start.19 = (f32[8,8,2]{2,1,0:T(8,128)S(1)}, f32[8,8,2]{2,1,0:T(8,128)S(1)}, u32[]{:S(2)}, u32[]{:S(2)}) collective-permute-start(f32[8,8,2]{2,1,0:T(8,128)S(1)} %get-tuple-element.140), channel_id=1, source_target_pairs={{64,0},{128,64},{192,128},{65,1},{129,65},{193,129},{66,2},{130,66... | collective-permute-start | bytes 1544 | tf_op jit(solution)/shard_map/ppermute | solution.py:21
  162.4 6.5 %collective-permute-start.22 = (f32[2,12,36]{2,1,0:T(8,128)S(1)}, f32[2,12,36]{2,1,0:T(8,128)S(1)}, u32[]{:S(2)}, u32[]{:S(2)}) collective-permute-start(f32[2,12,36]{2,1,0:T(8,128)S(1)} %get-tuple-element.138), channel_id=1, source_target_pairs={{1,0},{2,1},{3,2},{4,3},{5,4},{6,5},{7,6},{8,7},{9,8},{10,9},{11,1... | collective-permute-start | bytes 10376 | tf_op jit(solution)/shard_map/ppermute | solution.py:21
  165.6 6.6 %collective-permute-start.23 = (f32[2,12,36]{2,1,0:T(8,128)S(1)}, f32[2,12,36]{2,1,0:T(8,128)S(1)}, u32[]{:S(2)}, u32[]{:S(2)}) collective-permute-start(f32[2,12,36]{2,1,0:T(8,128)S(1)} %get-tuple-element.137), channel_id=1, source_target_pairs={{0,1},{1,2},{2,3},{3,4},{4,5},{5,6},{6,7},{7,8},{8,9},{9,10},{10,1... | collective-permute-start | bytes 10376 | tf_op jit(solution)/shard_map/ppermute | solution.py:20
  175.4 17.5 %collective-permute-start.24 = (f32[16,16,2]{2,1,0:T(8,128)S(1)}, f32[16,16,2]{2,1,0:T(8,128)S(1)}, u32[]{:S(2)}, u32[]{:S(2)}) collective-permute-start(f32[16,16,2]{2,1,0:T(8,128)S(1)} %get-tuple-element.123), channel_id=1, source_target_pairs={{0,64},{64,128},{128,192},{1,65},{65,129},{129,193},{2,66},{66,130... | collective-permute-start | bytes 6152 | tf_op jit(solution)/shard_map/ppermute | solution.py:20
  179.9 13.0 %collective-permute-start.25 = (f32[16,16,2]{2,1,0:T(8,128)S(1)}, f32[16,16,2]{2,1,0:T(8,128)S(1)}, u32[]{:S(2)}, u32[]{:S(2)}) collective-permute-start(f32[16,16,2]{2,1,0:T(8,128)S(1)} %get-tuple-element.124), channel_id=1, source_target_pairs={{64,0},{128,64},{192,128},{65,1},{129,65},{193,129},{66,2},{130,66... | collective-permute-start | bytes 6152 | tf_op jit(solution)/shard_map/ppermute | solution.py:21
  193.0 10.0 %collective-permute-start.27 = (f32[16,2,68]{2,0,1:T(8,128)S(1)}, f32[16,2,68]{2,0,1:T(8,128)S(1)}, u32[]{:S(2)}, u32[]{:S(2)}) collective-permute-start(f32[16,2,68]{2,0,1:T(8,128)S(1)} %copy.203), channel_id=1, source_target_pairs={{16,0},{32,16},{48,32},{17,1},{33,17},{49,33},{18,2},{34,18},{50,3... | collective-permute-start | bytes 26120 | tf_op jit(solution)/shard_map/ppermute | solution.py:21
  194.3 8.7 %collective-permute-start.26 = (f32[16,2,68]{2,0,1:T(8,128)S(1)}, f32[16,2,68]{2,0,1:T(8,128)S(1)}, u32[]{:S(2)}, u32[]{:S(2)}) collective-permute-start(f32[16,2,68]{2,0,1:T(8,128)S(1)} %copy.202), channel_id=1, source_target_pairs={{0,16},{16,32},{32,48},{1,17},{17,33},{33,49},{2,18},{18,34},{34,5... | collective-permute-start | bytes 26120 | tf_op jit(solution)/shard_map/ppermute | solution.py:20
  203.2 10.6 %collective-permute-start.28 = (f32[2,20,68]{2,1,0:T(8,128)S(1)}, f32[2,20,68]{2,1,0:T(8,128)S(1)}, u32[]{:S(2)}, u32[]{:S(2)}) collective-permute-start(f32[2,20,68]{2,1,0:T(8,128)S(1)} %get-tuple-element.122), channel_id=1, source_target_pairs={{1,0},{2,1},{3,2},{4,3},{5,4},{6,5},{7,6},{8,7},{9,8},{10,9},{11,1... | collective-permute-start | bytes 32648 | tf_op jit(solution)/shard_map/ppermute | solution.py:21
  210.5 6.7 %collective-permute-start.29 = (f32[2,20,68]{2,1,0:T(8,128)S(1)}, f32[2,20,68]{2,1,0:T(8,128)S(1)}, u32[]{:S(2)}, u32[]{:S(2)}) collective-permute-start(f32[2,20,68]{2,1,0:T(8,128)S(1)} %get-tuple-element.121), channel_id=1, source_target_pairs={{0,1},{1,2},{2,3},{3,4},{4,5},{5,6},{6,7},{7,8},{8,9},{9,10},{10,1... | collective-permute-start | bytes 32648 | tf_op jit(solution)/shard_map/ppermute | solution.py:20
  (76 other events, 902.1 us)
where the time goes:
time: 223 us; the launch traced here: 222 us
  starting transfers between devices  108 us (48%)
  local copies, waits for them, and re-layouts  40.7 us (18%)
  waiting for transfers between devices  40.3 us (18%)
  other arithmetic  31.7 us (14%)
    ppermute x15, starting transfers between devices, extended(): before = lax.ppermute(last, axis, up)  69.5 us
    ppermute x15, starting transfers between devices, extended(): after = lax.ppermute(initial, axis, down)  38.2 us
    ppermute x15, waiting for transfers between devices, extended(): after = lax.ppermute(initial, axis, down)  22.9 us
    ppermute x15, waiting for transfers between devices, extended(): before = lax.ppermute(last, axis, up)  17.5 us
    add x6, other arithmetic, convolve_axis(): summed + kernel_rows[:, offset].reshape(weight_shape) * lax.slice_in_dim(...  16.9 us
    slice x20, local copies, waits for them, and re-layouts, restrict_axis(): lax.slice_in_dim(padded, first, first + 2 * count - 1, stride=2, axis=axi...  15.5 us
    mul x3, local copies, waits for them, and re-layouts, convolve_axis(): kernel_rows[:, 0].reshape(weight_shape)  9.56 us
    reduce_sum x3, other arithmetic, stencil_box(): return jnp.sum(smoothed, axis=0)  6.91 us
  transfers between devices with their start and end apart: 30, of which 12 were waited for; matrix products, arithmetic and copies ran while one was open for 18% of the time, Pallas kernels for 0%

commit v1 on v0

v1 whole, which is shorter than its diff:
```python
import functools

import jax
import jax.numpy as jnp
from jax import lax
from jax.experimental import pallas as pl
from jax.experimental.pallas import tpu as pltpu
from jax.sharding import PartitionSpec as P

F32, BF16 = jnp.float32, jnp.bfloat16
MESH = pl.DeviceIdType.MESH
HI_LANE, LO_LANE = 80, 88
NOWHERE = -10000

SIZES = ((32, 32, 128), (16, 16, 64), (8, 8, 32))
LEVELS = (
    dict(planes=48, rows=48, keep=48, own=(8, 32), z={0: (8, 8, 32), 1: (32, 0, 8), -1: (8, 40, 8)},
         y={0: (8, 8, 32), 1: (32, 0, 8), -1: (8, 40, 8)}, tiles=((8, 32),), packrows=32, groups=2,
         py={0: (0, 8, 32), 1: (24, 0, 8), -1: (0, 40, 8)}, pg={0: (0, 1, 2), 1: (1, 0, 1), -1: (0, 3, 1)},
         face=(120, 0), runs=((0, 8, 0, 8), (8, 16, 1, 0), (24, 16, 2, 0), (40, 8, 3, 0))),
    dict(planes=35, rows=48, keep=48, own=(7, 21), z={0: (7, 7, 21), 1: (16, 0, 7), -1: (12, 28, 7)},
         y={0: (8, 8, 24), 1: (16, 0, 8), -1: (40, 32, 8)}, tiles=((8, 24), (40, 8)), packrows=32, groups=2,
         py={0: (0, 8, 24), 1: (8, 0, 8), -1: (24, 32, 8)}, pg={0: (0, 1, 2), 1: (0, 0, 1), -1: (0, 3, 1)},
         face=(56, 5), runs=((0, 7, 0, 9), (7, 16, 1, 0), (23, 5, 2, 0), (28, 7, 3, 5))),
    dict(planes=29, rows=40, keep=32, own=(7, 15), z={0: (7, 7, 15), 1: (8, 0, 7), -1: (14, 22, 7)},
         y={0: (8, 8, 16), 1: (8, 0, 8), -1: (32, 24, 8)}, tiles=((8, 16), (32, 8)), packrows=24, groups=1,
         py={0: (0, 8, 16), 1: (0, 0, 8), -1: (16, 24, 8)}, pg={0: (0, 1, 1), 1: (0, 0, 1), -1: (0, 2, 1)},
         face=(24, 7), runs=((0, 7, 0, 1), (7, 15, 1, 0), (22, 7, 2, 7))),
)
STEPS = tuple((dz, dy, dx) for dx in (1, -1, 0) for dy in (1, -1, 0) for dz in (1, -1, 0) if (dz, dy, dx) != (0, 0, 0))


def split(x):
    high = x.astype(BF16)
    return high, (x - high.astype(F32)).astype(BF16)


def iota(shape, axis):
    return lax.broadcasted_iota(jnp.int32, shape, axis)


def pick(condition, value, other):
    return jnp.where(condition, value, other)


def dot(a, b):
    return jnp.dot(a, b, preferred_element_type=F32)


def exact(a, b):
    return jnp.dot(a, b, preferred_element_type=F32, precision=lax.Precision.HIGHEST)


def weight(d):
    d = jnp.abs(d)
    return pick(d == 0, 1.0, pick(d == 1, 0.5625, pick(d == 3, -0.0625, 0.0))).astype(F32)


def band(diff, row):
    total = jnp.zeros(diff.shape, F32)
    for k in range(17):
        total = pick(diff == k - 8, row[k], total)
    return total


def x_coords(slot, level):
    if level == 0:
        base, hi, lo, first, tile = 128, 128, -8, 0, 128
    elif level == 1:
        base, hi, lo, first, tile = 69, 67, -10, -2, 0
    else:
        base, hi, lo, first, tile = 39, 36, -11, -3, 0
    coord = pick(slot < base, slot + first, NOWHERE)
    h, l = slot - tile - HI_LANE, slot - tile - LO_LANE
    coord = pick((h >= 0) & (h < 8), h + hi, coord)
    return pick((l >= 0) & (l < 8), l + lo, coord)


def y_coords(row, level):
    if level == 0:
        return row - 8
    if level == 1:
        coord = pick(row < 8, row - 10, pick(row < 29, row - 10, NOWHERE))
        return pick((row >= 32) & (row < 40), row - 32 + 19, coord)
    coord = pick(row < 8, row - 11, pick(row < 23, row - 11, NOWHERE))
    return pick((row >= 24) & (row < 32), row - 24 + 12, coord)


def kernel(counts, q_hbm, taps, out, *scratch):
    (e0, e1, e2, px0, px1, px2, pk0, pk1, pk2, l0h, l0l, l1h, l1l, l2h, l2l, a1, a2, f0, h1, b1, b2, c2,
     s0, s1, s2, x0h, x0l, xr1, x1h, x1l, xr2, x2h, x2l, yr1, yr2, y0, y1, y2,
     local_sem, send_sem, recv_sem) = scratch
    ext, halo, pack = (e0, e1, e2), (px0, px1, px2), (pk0, pk1, pk2)
    nz, ny, nx = counts
    gz, gy, gx = lax.axis_index("gz"), lax.axis_index("gy"), lax.axis_index("gx")

    def tap_row(level, term):
        return [taps[level, term, k] for k in range(17)]

    def neighbour(step, sign):
        dz, dy, dx = (sign * s for s in step)
        z, y, x = gz + dz, gy + dy, gx + dx
        here = None
        for d, v, n in ((dz, z, nz), (dy, y, ny), (dx, x, nx)):
            test = v < n if d > 0 else (v >= 0 if d < 0 else None)
            if test is not None:
                here = test if here is None else here & test
        return here, {"gz": z, "gy": y, "gx": x}

    load = pltpu.make_async_copy(q_hbm, e0.at[pl.ds(8, 32), pl.ds(8, 32), :], local_sem)
    load.start()

    def clear(i, _):
        zero = jnp.zeros((8, 128), F32)
        for row in range(0, 48, 8):
            e0[i, row : row + 8, :] = zero
            e0[40 + i, row : row + 8, :] = zero
        return 0

    lax.fori_loop(0, 8, clear, 0)

    def clear_sides(i, _):
        zero = jnp.zeros((8, 128), F32)
        e0[8 + i, 0:8, :] = zero
        e0[8 + i, 40:48, :] = zero
        return 0

    lax.fori_loop(0, 32, clear_sides, 0)

    def clear_planes(ref):
        def body(i, _):
            ref[i] = jnp.zeros(ref.shape[1:], F32)
            return 0

        lax.fori_loop(0, ref.shape[0], body, 0)

    clear_planes(e1)
    clear_planes(e2)
    for ref in halo:
        for side in range(2):
            for g in range(ref.shape[1]):
                ref[side, g] = jnp.zeros(ref.shape[2:], F32)

    barrier = pltpu.get_barrier_semaphore()
    for step in STEPS:
        here, device = neighbour(step, 1)

        @pl.when(here)
        def _():
            pl.semaphore_signal(barrier, inc=1, device_id=device, device_id_type=MESH)

    def pack_faces(level):
        lv, src = LEVELS[level], ext[level]
        start, planes = lv["own"]
        lane = iota((lv["packrows"], 128), 1) // 8
        for g in range(lv["groups"]):
            faces = [jnp.zeros((lv["packrows"], 128), F32) for _ in range(2)]
            for j in range(min(16, planes - 16 * g)):
                parts = [src[start + 16 * g + j, r : r + n, :] for r, n in lv["tiles"]]
                v = parts[0] if len(parts) == 1 else jnp.concatenate(parts, axis=0)
                for f in range(2):
                    faces[f] = pick(lane == j, pltpu.roll(v, (8 * j - lv["face"][f]) % 128, 1), faces[f])
            for f in range(2):
                pack[level][f, g] = faces[f]

    def copies(level):
        lv = LEVELS[level]
        result = []
        for index, step in enumerate(STEPS):
            dz, dy, dx = step
            target, device = neighbour(step, 1)
            source, _ = neighbour(step, -1)
            if dx == 0:
                z, y = lv["z"][dz], lv["y"][dy]
                src = ext[level].at[pl.ds(z[0], z[2]), pl.ds(y[0], y[2]), :]
                dst = ext[level].at[pl.ds(z[1], z[2]), pl.ds(y[1], y[2]), :]
            else:
                side = 0 if dx == 1 else 1
                z, y = lv["pg"][dz], lv["py"][dy]
                src = pack[level].at[side, pl.ds(z[0], z[2]), pl.ds(y[0], y[2]), :]
                dst = halo[level].at[side, pl.ds(z[1], z[2]), pl.ds(y[1], y[2]), :]
            copy = pltpu.make_async_remote_copy(
                src_ref=src, dst_ref=dst, send_sem=send_sem.at[level, index], recv_sem=recv_sem.at[level, index],
                device_id=device, device_id_type=MESH)
            result.append((target, source, copy))
        return result

    def send(level):
        for target, _, copy in copies(level):
            @pl.when(target)
            def _():
                copy.start()

    def receive(level):
        for _, source, copy in copies(level):
            @pl.when(source)
            def _():
                copy.wait_recv()

    def finish(level):
        for target, _, copy in copies(level):
            @pl.when(target)
            def _():
                copy.wait_send()

    def unpack(level, lh, ll):
        lv = LEVELS[level]
        rows = lv["keep"]
        lane = iota((rows, 128), 1)
        is_hi, is_lo = (lane >= HI_LANE) & (lane < HI_LANE + 8), (lane >= LO_LANE) & (lane < LO_LANE + 8)
        for first, count, g, j0 in lv["runs"]:
            for i in range(count):
                e, j = first + i, j0 + i
                low = pltpu.roll(halo[level][0, g], (LO_LANE - 8 * j) % 128, 1)
                high = pltpu.roll(halo[level][1, g], (HI_LANE - 8 * j) % 128, 1)
                v = ext[level][e, 0:rows, :]
                if level == 0:
                    side = pick(is_hi, high, pick(is_lo, low, 0.0))
                    lh[e, :, 0:128], ll[e, :, 0:128] = split(v)
                    lh[e, :, 128:256], ll[e, :, 128:256] = split(side)
                else:
                    v = pick(is_hi, high, pick(is_lo, low, v))
                    lh[e], ll[e] = split(v)

    load.wait()
    pack_faces(0)

    reach = [1 + jnp.minimum(g, 1) + jnp.minimum(n - 1 - g, 1) for g, n in ((gz, nz), (gy, ny), (gx, nx))]
    pl.semaphore_wait(barrier, reach[0] * reach[1] * reach[2] - 1)
    send(0)

    def inside(coord, g, n, count):
        return (coord + g * n >= 0) & (coord + g * n < n * count)

    for t in range(2):
        x0h[:, 128 * t : 128 * (t + 1)], x0l[:, 128 * t : 128 * (t + 1)] = split(
            band(x_coords(iota((256, 128), 0), 0) - iota((256, 128), 1), tap_row(0, t)))
    m = iota((256, 128), 1) - 2
    xr1[...] = pick((m < 67) & inside(m, gx, 64, nx), weight(x_coords(iota((256, 128), 0), 0) - 2 * m), 0.0).astype(BF16)
    c = iota((128, 128), 1) - 3
    xr2[...] = pick((c < 36) & inside(c, gx, 32, nx), weight(x_coords(iota((128, 128), 0), 1) - 2 * c), 0.0).astype(BF16)
    sq = (128, 128)
    row, col = iota(sq, 0), iota(sq, 1)
    m_col, m_row, c_col, c_row = col - 1, row - 1, col - 2, row - 2
    up1 = weight(col - 2 * m_row)
    up1 = pick(m_row < 66, up1, 0.0)
    up2 = pick((c_row < 35) & (m_col < 66) & inside(m_col, gx, 64, nx), weight(m_col - 2 * c_row), 0.0)
    up21 = exact(up2, up1)
    for t in range(2):
        k1 = pick((m_col < 66) & inside(m_col, gx, 64, nx), band(x_coords(row, 1) - m_col, tap_row(1, t)), 0.0)
        x1h[:, 128 * t : 128 * (t + 1)], x1l[:, 128 * t : 128 * (t + 1)] = split(exact(k1, up1))
        k2 = pick((c_col < 35) & inside(c_col, gx, 32, nx), band(x_coords(row, 2) - c_col, tap_row(2, t)), 0.0)
        x2h[:, 128 * t : 128 * (t + 1)], x2l[:, 128 * t : 128 * (t + 1)] = split(exact(k2, up21))

    row, col = iota((32, 128), 0), iota((32, 128), 1)
    m = pick(row < 24, row - 2, row - 24 + 3)
    yr1[...] = pick((m < 19) & inside(m, gy, 16, ny), weight(y_coords(col, 0) - 2 * m), 0.0).astype(BF16)
    row, col = iota((24, 128), 0), iota((24, 128), 1)
    c = pick(row < 16, row - 3, row - 16 + 4)
    yr2[...] = pick((c < 12) & inside(c, gy, 8, ny), weight(y_coords(col, 1) - 2 * c), 0.0).astype(BF16)

    def band_pair(coord, centre, second, level):
        rows = [jnp.where(second, taps[level, 1, k], taps[level, 0, k]) for k in range(17)]
        return band(coord - centre, rows)

    row, col = iota((32, 128), 0), iota((32, 128), 1)
    y0[0:32], y0[32:64] = split(band_pair(y_coords(pick(col >= 48, col - 48, col), 0), row, col >= 48, 0))
    m_col = col - 1
    yup1 = pick(m_col < 18, weight(row - 2 * m_col), 0.0)
    row, col = iota(sq, 0), iota(sq, 1)
    m_row, c_col, c_row = row - 1, col - 2, row - 2
    yup2 = pick((m_row < 18) & inside(m_row, gy, 16, ny) & (c_col < 11), weight(m_row - 2 * c_col), 0.0)
    k1 = band_pair(y_coords(pick(col >= 48, col - 48, col), 1), m_row, col >= 48, 1)
    k1 = pick((m_row < 18) & inside(m_row, gy, 16, ny) & (col < 96), k1, 0.0)
    y1[0:32], y1[32:64] = split(exact(yup1, k1))
    k2 = band_pair(y_coords(pick(col >= 32, col - 32, col), 2), c_row, col >= 32, 2)
    k2 = pick((c_row < 11) & inside(c_row, gy, 8, ny) & (col < 64), k2, 0.0)
    y2[0:32], y2[32:64] = split(exact(exact(yup1, yup2), k2))

    z_low = jnp.where(gz > 0, 1.0, 0.0).astype(F32)
    z_high = jnp.where(gz < nz - 1, 1.0, 0.0).astype(F32)

    def edge(v, low, high):
        n = v.shape[0]
        return jnp.concatenate([v[:low] * z_low, v[low : n - high], v[n - high :] * z_high], axis=0)

    def lanes(ref, first, count):
        return jnp.concatenate([ref[first + i] for i in range(count)], axis=1)

    def two(lh, ll, matrix):
        return dot(lh, matrix) + dot(ll, matrix)

    def three(lh, ll, high, low):
        return dot(lh, high) + dot(ll, high) + dot(lh, low)

    receive(0)
    unpack(0, l0h, l0l)

    def restrict_x(i, _):
        lh, ll = (r[pl.ds(8 * i, 8)].reshape(384, 256) for r in (l0h, l0l))
        a1[pl.ds(4 * i, 4)] = two(lh, ll, xr1[...]).reshape(4, 2, 48, 128)
        return 0

    lax.fori_loop(0, 6, restrict_x, 0)

    def restrict_z(i, _):
        rows = pl.ds(pl.multiple_of(8 * i, 8), 8)
        even, odd = a1[:, 0, rows, :], a1[:, 1, rows, :]
        v = even[2:23] + 0.5625 * (odd[1:22] + odd[2:23]) - 0.0625 * (odd[0:21] + odd[3:24])
        a2[:, rows, :] = edge(v, 2, 3)
        return 0

    lax.fori_loop(0, 6, restrict_z, 0)
    for p in range(0, 21, 7):
        high, low = split(lanes(a2, p, 7))
        v = dot(yr1[:, 0:48], high) + dot(yr1[:, 0:48], low)
        for i in range(7):
            piece = v[:, 128 * i : 128 * (i + 1)]
            e1[7 + p + i, 8:32, :] = piece[0:24]
            e1[7 + p + i, 40:48, :] = piece[24:32]
    pack_faces(1)
    send(1)

    def conv_x0(i, _):
        lh, ll = (r[pl.ds(8 * i, 8)].reshape(384, 256) for r in (l0h, l0l))
        for t in range(2):
            cols = slice(128 * t, 128 * (t + 1))
            f0[t, pl.ds(8 * i, 8)] = three(lh, ll, x0h[:, cols], x0l[:, cols]).reshape(8, 48, 128)
        return 0

    lax.fori_loop(0, 6, conv_x0, 0)

    def conv_z(field, level, t, rows, count):
        total = taps[level, t, 0] * field[t, 0:count, rows, :]
        for k in range(1, 17):
            total = total + taps[level, t, k] * field[t, k : k + count, rows, :]
        return total

    def conv_z0(i, _):
        rows = pl.ds(pl.multiple_of(8 * i, 8), 8)
        for t in range(2):
            s0[:, pl.ds(pl.multiple_of(48 * t + 8 * i, 8), 8), :] = conv_z(f0, 0, t, rows, 32)
        return 0

    lax.fori_loop(0, 6, conv_z0, 0)

    receive(1)
    unpack(1, l1h, l1l)
    l1h[35] = jnp.zeros((48, 128), BF16)
    l1l[35] = jnp.zeros((48, 128), BF16)

    def restrict_x1(i, _):
        lh, ll = (r[pl.ds(6 * i, 6)].reshape(288, 128) for r in (l1h, l1l))
        b1[pl.ds(3 * i, 3)] = two(lh, ll, xr2[...]).reshape(3, 2, 48, 128)
        return 0

    lax.fori_loop(0, 6, restrict_x1, 0)

    def restrict_z1(i, _):
        rows = pl.ds(pl.multiple_of(8 * i, 8), 8)
        even, odd = b1[:, 0, rows, :], b1[:, 1, rows, :]
        v = odd[1:16] + 0.5625 * (even[1:16] + even[2:17]) - 0.0625 * (even[0:15] + even[3:18])
        b2[:, rows, :] = edge(v, 3, 4)
        return 0

    lax.fori_loop(0, 6, restrict_z1, 0)
    for p in range(0, 15, 5):
        high, low = split(lanes(b2, p, 5))
        v = dot(yr2[:, 0:48], high) + dot(yr2[:, 0:48], low)
        for i in range(5):
            piece = v[:, 128 * i : 128 * (i + 1)]
            e2[7 + p + i, 8:24, :] = piece[0:16]
            e2[7 + p + i, 32:40, :] = piece[16:24]
    pack_faces(2)
    send(2)

    def conv_x1(i, _):
        lh, ll = (r[pl.ds(6 * i, 6)].reshape(288, 128) for r in (l1h, l1l))
        for t in range(2):
            cols = slice(128 * t, 128 * (t + 1))
            h1[t, pl.ds(6 * i, 6)] = three(lh, ll, x1h[:, cols], x1l[:, cols]).reshape(6, 48, 128)
        return 0

    lax.fori_loop(0, 6, conv_x1, 0)

    def refine(g, n):
        even = g[1 : n + 1]
        odd = 0.5625 * (even + g[2 : n + 2]) - 0.0625 * (g[0:n] + g[3 : n + 3])
        return even, odd

    def conv_z1(i, _):
        rows = pl.ds(pl.multiple_of(8 * i, 8), 8)
        for t in range(2):
            even, odd = refine(edge(conv_z(h1, 1, t, rows, 19), 1, 2), 16)
            target = pl.ds(pl.multiple_of(48 * t + 8 * i, 8), 8)
            s1[:, 0, target, :] = even
            s1[:, 1, target, :] = odd
        return 0

    lax.fori_loop(0, 6, conv_z1, 0)

    def apply_y(matrix, depth, planes):
        high, low = split(jnp.concatenate(planes, axis=1))
        both = dot(matrix[:, 0:depth], high)
        return both[0:32] + both[32:64] + dot(matrix[0:32, 0:depth], low)

    def merge(i, _):
        v = apply_y(y0, 96, [s0[4 * i + k] for k in range(4)])
        v = v + apply_y(y1, 96, [s1[2 * i + k // 2, k % 2] for k in range(4)])
        for k in range(4):
            out[4 * i + k] = v[:, 128 * k : 128 * (k + 1)]
        return 0

    lax.fori_loop(0, 8, merge, 0)

    receive(2)
    unpack(2, l2h, l2l)
    for e in range(29, 32):
        l2h[e] = jnp.zeros((32, 128), BF16)
        l2l[e] = jnp.zeros((32, 128), BF16)

    def conv_x2(i, _):
        lh, ll = (r[pl.ds(8 * i, 8)].reshape(256, 128) for r in (l2h, l2l))
        for t in range(2):
            cols = slice(128 * t, 128 * (t + 1))
            c2[t, pl.ds(8 * i, 8)] = three(lh, ll, x2h[:, cols], x2l[:, cols]).reshape(8, 32, 128)
        return 0

    lax.fori_loop(0, 4, conv_x2, 0)

    def conv_z2(i, _):
        rows = pl.ds(pl.multiple_of(8 * i, 8), 8)
        for t in range(2):
            h = edge(conv_z(c2, 2, t, rows, 13), 2, 3)
            even = h[2:11]
            odd = 0.5625 * (h[1:11] + h[2:12]) - 0.0625 * (h[0:10] + h[3:13])
            g = []
            for k in range(9):
                g += [odd[k : k + 1], even[k : k + 1]]
            even, odd = refine(edge(jnp.concatenate(g + [odd[9:10]], axis=0), 1, 2), 16)
            target = pl.ds(pl.multiple_of(32 * t + 8 * i, 8), 8)
            s2[:, 0, target, :] = even
            s2[:, 1, target, :] = odd
        return 0

    lax.fori_loop(0, 4, conv_z2, 0)

    def add_coarse(i, _):
        v = apply_y(y2, 64, [s2[2 * i + k // 2, k % 2] for k in range(4)])
        for k in range(4):
            out[4 * i + k] = out[4 * i + k] + v[:, 128 * k : 128 * (k + 1)]
        return 0

    lax.fori_loop(0, 8, add_coarse, 0)

    for level in range(3):
        finish(level)


def solution(mesh):
    counts = tuple(mesh.shape[a] for a in ("gz", "gy", "gx"))

    def local(charges, kernel_taps):
        vm = pltpu.VMEM
        scratch = [
            vm((48, 48, 128), F32), vm((35, 48, 128), F32), vm((29, 40, 128), F32),
            vm((2, 4, 48, 128), F32), vm((2, 4, 48, 128), F32), vm((2, 3, 32, 128), F32),
            vm((2, 2, 32, 128), F32), vm((2, 2, 32, 128), F32), vm((2, 1, 24, 128), F32),
            vm((48, 48, 256), BF16), vm((48, 48, 256), BF16),
            vm((36, 48, 128), BF16), vm((36, 48, 128), BF16),
            vm((32, 32, 128), BF16), vm((32, 32, 128), BF16),
            vm((24, 2, 48, 128), F32), vm((21, 48, 128), F32),
            vm((2, 48, 48, 128), F32), vm((2, 36, 48, 128), F32),
            vm((18, 2, 48, 128), F32), vm((15, 48, 128), F32), vm((2, 32, 32, 128), F32),
            vm((32, 96, 128), F32), vm((16, 2, 96, 128), F32), vm((16, 2, 64, 128), F32),
            vm((256, 256), BF16), vm((256, 256), BF16), vm((256, 128), BF16),
            vm((128, 256), BF16), vm((128, 256), BF16), vm((128, 128), BF16),
            vm((128, 256), BF16), vm((128, 256), BF16),
            vm((32, 128), BF16), vm((24, 128), BF16),
            vm((64, 128), BF16), vm((64, 128), BF16), vm((64, 128), BF16),
            pltpu.SemaphoreType.DMA, pltpu.SemaphoreType.DMA((3, 26)), pltpu.SemaphoreType.DMA((3, 26)),
        ]
        return pl.pallas_call(
            functools.partial(kernel, counts),
            out_shape=jax.ShapeDtypeStruct((32, 32, 128), F32),
            in_specs=[pl.BlockSpec(memory_space=pl.ANY), pl.BlockSpec(memory_space=pltpu.SMEM)],
            out_specs=pl.BlockSpec(memory_space=pltpu.VMEM),
            scratch_shapes=scratch,
            compiler_params=pltpu.CompilerParams(
                collective_id=0, has_side_effects=True, vmem_limit_bytes=56 * 1024 * 1024),
        )(charges, kernel_taps)

    return jax.shard_map(
        local, mesh=mesh, in_specs=(P("gz", "gy", "gx"), P()), out_specs=P("gz", "gy", "gx"), check_vma=False)
```

time: 223 us -> 42.8 us (0.19)
  starting transfers between devices: 108 us -> 0 us
  Pallas kernels: 0 us -> 40.7 us
  waiting for transfers between devices: 40.3 us -> 0 us
  local copies, waits for them, and re-layouts: 40.7 us -> 1.87 us
  other arithmetic: 31.7 us -> 0 us
    ppermute x30 -> x0, starting transfers between devices: 108 us -> none  [the longest x15 69.5 us: extended(): before = lax.ppermute(last, axis, up)]
    pallas_call x0 -> x1, Pallas kernels: none -> 40.7 us  [local(): pl.pallas_call(functools.partial(kernel, counts), out_shape=jax.ShapeDtyp...]
    ppermute x30 -> x0, waiting for transfers between devices: 40.3 us -> none  [the longest x15 22.9 us: extended(): after = lax.ppermute(initial, axis, down)]
    slice x36 -> x0, local copies, waits for them, and re-layouts: 20.3 us -> none  [the longest x20 15.5 us: restrict_axis(): lax.slice_in_dim(padded, first, first + 2 * count - 1, stride=2, axis=axi...]
    add x14 -> x0, other arithmetic: 18.2 us -> none  [the longest x6 16.9 us: convolve_axis(): summed + kernel_rows[:, offset].reshape(weight_shape) * lax.slice_in_dim(...]
    mul x3 -> x0, local copies, waits for them, and re-layouts: 9.56 us -> none  [convolve_axis(): kernel_rows[:, 0].reshape(weight_shape)]
    reduce_sum x3 -> x0, other arithmetic: 6.91 us -> none  [stencil_box(): return jnp.sum(smoothed, axis=0)]
    another operation x6 -> x0, local copies, waits for them, and re-layouts: 3.32 us -> none  [prolong_axis(): stacked = jnp.stack([centre, odd_cells], axis=axis_dim + 1)]
  transfers between devices with their start and end apart: 30 -> 0, of which waited for: 12 -> 0; matrix products, arithmetic and copies ran while one was open for 18% -> 0% of each run, Pallas kernels for 0% -> 0%
where the time goes in v1:
time: 42.8 us; the launch traced here: 42.6 us
  Pallas kernels  40.7 us (95%)
  local copies, waits for them, and re-layouts  1.87 us (4%)
    pallas_call x1, Pallas kernels, local(): pl.pallas_call(functools.partial(kernel, counts), out_shape=jax.ShapeDtyp...  40.7 us
    unnamed x1, local copies, waits for them, and re-layouts  1.87 us

profile of v1, /device:TPU:7, one launch (start us, length us, event | category | flops | bytes accessed | tf_op | source)
XLA Modules:
  0.0 42.6 jit_solution(6525743093850532396)
XLA Ops:
  0.0 40.7 %shard_map.28 = f32[32,32,128]{2,1,0:T(8,128)} custom-call(f32[32,32,128]{2,1,0:T(8,128)} %q_hbm.1, f32[3,2,17]{2,1,0:T(2,128)} %taps.1), custom_call_target="tpu_custom_call" | custom-call | tf_op jit(solution)/shard_map/pallas_call | solution.py:483
  40.7 1.9 %copy.4 = f32[32,32,128]{2,1,0:T(8,128)} copy(f32[32,32,128]{2,1,0:T(8,128)} %shard_map.28) | data formatting | bytes 1048576

commit v2 on v1

v2 whole, which is shorter than its diff:
```python
import functools

import jax
import jax.numpy as jnp
from jax import lax
from jax.experimental import pallas as pl
from jax.experimental.pallas import tpu as pltpu
from jax.sharding import PartitionSpec as P

F32, BF16 = jnp.float32, jnp.bfloat16
MESH = pl.DeviceIdType.MESH
NOWHERE = -10000

LEVELS = (
    dict(keep=48, own=(8, 32), z={0: (8, 8, 32), 1: (32, 0, 8), -1: (8, 40, 8)},
         y={0: (8, 8, 32), 1: (32, 0, 8), -1: (8, 40, 8)}, tiles=((8, 32),), packrows=32, groups=2, lanes=(80, 88),
         py={0: (0, 8, 32), 1: (24, 0, 8), -1: (0, 40, 8)}, pg={0: (0, 1, 2), 1: (1, 0, 1), -1: (0, 3, 1)},
         face=(120, 0), runs=((0, 8, 0, 8), (8, 16, 1, 0), (24, 16, 2, 0), (40, 8, 3, 0))),
    dict(keep=40, own=(7, 21), z={0: (7, 7, 21), 1: (16, 0, 7), -1: (12, 28, 7)},
         y={0: (8, 8, 24), 1: (16, 0, 8), -1: (40, 32, 8)}, tiles=((8, 24), (40, 8)), packrows=32, groups=2, lanes=(80, 88),
         py={0: (0, 8, 24), 1: (8, 0, 8), -1: (24, 32, 8)}, pg={0: (0, 1, 2), 1: (0, 0, 1), -1: (0, 3, 1)},
         face=(56, 5), runs=((0, 7, 0, 9), (7, 16, 1, 0), (23, 5, 2, 0), (28, 7, 3, 5))),
    dict(keep=32, own=(7, 15), z={0: (7, 7, 15), 1: (8, 0, 7), -1: (14, 22, 7)},
         y={0: (8, 8, 16), 1: (8, 0, 8), -1: (32, 24, 8)}, tiles=((8, 16), (32, 8)), packrows=24, groups=1, lanes=(40, 48),
         py={0: (0, 8, 16), 1: (0, 0, 8), -1: (16, 24, 8)}, pg={0: (0, 1, 1), 1: (0, 0, 1), -1: (0, 2, 1)},
         face=(24, 7), runs=((0, 7, 0, 1), (7, 15, 1, 0), (22, 7, 2, 7))),
)
STEPS = tuple((dz, dy, dx) for dx in (1, -1, 0) for dy in (1, -1, 0) for dz in (1, -1, 0) if (dz, dy, dx) != (0, 0, 0))


def split(x):
    high = x.astype(BF16)
    return high, (x - high.astype(F32)).astype(BF16)


def iota(shape, axis):
    return lax.broadcasted_iota(jnp.int32, shape, axis)


def pick(condition, value, other):
    return jnp.where(condition, value, other)


def dot(a, b):
    return jnp.dot(a, b, preferred_element_type=F32)


def exact(a, b):
    return jnp.dot(a, b, preferred_element_type=F32, precision=lax.Precision.HIGHEST)


def weight(d):
    d = jnp.abs(d)
    return pick(d == 0, 1.0, pick(d == 1, 0.5625, pick(d == 3, -0.0625, 0.0))).astype(F32)


def band(diff, row):
    total = jnp.zeros(diff.shape, F32)
    for k in range(17):
        total = pick(diff == k - 8, row[k], total)
    return total


def x_coords(slot, level):
    if level == 0:
        base, hi, lo, first, tile = 128, 128, -8, 0, 128
    elif level == 1:
        base, hi, lo, first, tile = 69, 67, -10, -2, 0
    else:
        base, hi, lo, first, tile = 39, 36, -11, -3, 0
    coord = pick(slot < base, slot + first, NOWHERE)
    h, l = slot - tile - LEVELS[level]["lanes"][0], slot - tile - LEVELS[level]["lanes"][1]
    coord = pick((h >= 0) & (h < 8), h + hi, coord)
    return pick((l >= 0) & (l < 8), l + lo, coord)


def y_coords(row, level):
    if level == 0:
        return row - 8
    if level == 1:
        coord = pick(row < 8, row - 10, pick(row < 29, row - 10, NOWHERE))
        return pick((row >= 32) & (row < 40), row - 32 + 19, coord)
    coord = pick(row < 8, row - 11, pick(row < 23, row - 11, NOWHERE))
    return pick((row >= 24) & (row < 32), row - 24 + 12, coord)


def kernel(counts, q_hbm, taps_hbm, out, *scratch):
    (e0, e1, e2, px0, px1, px2, pk0, pk1, pk2, side, v1, v2, r0, r1, f0, s0, z1, q1h, q1l, t1, z2, t2,
     x0, xr1, x1, xr2, x2, yr1, yr2, y0, y1, y2, taps, local_sem, taps_sem, send_sem, recv_sem) = scratch
    ext, halo, pack = (e0, e1, e2), (px0, px1, px2), (pk0, pk1, pk2)
    nz, ny, nx = counts
    gz, gy, gx = lax.axis_index("gz"), lax.axis_index("gy"), lax.axis_index("gx")

    def neighbour(step, sign):
        dz, dy, dx = (sign * s for s in step)
        z, y, x = gz + dz, gy + dy, gx + dx
        here = None
        for d, v, n in ((dz, z, nz), (dy, y, ny), (dx, x, nx)):
            test = v < n if d > 0 else (v >= 0 if d < 0 else None)
            if test is not None:
                here = test if here is None else here & test
        return here, {"gz": z, "gy": y, "gx": x}

    load = pltpu.make_async_copy(q_hbm, e0.at[pl.ds(8, 32), pl.ds(8, 32), :], local_sem)
    load.start()
    load_taps = pltpu.make_async_copy(taps_hbm, taps, taps_sem)
    load_taps.start()

    barrier = pltpu.get_barrier_semaphore()
    for step in STEPS:
        here, device = neighbour(step, 1)

        @pl.when(here)
        def _():
            pl.semaphore_signal(barrier, inc=1, device_id=device, device_id_type=MESH)

    def places(level, step):
        lv = LEVELS[level]
        dz, dy, dx = step
        if dx == 0:
            z, y = lv["z"][dz], lv["y"][dy]
            src = ext[level].at[pl.ds(z[0], z[2]), pl.ds(y[0], y[2]), :]
            dst = ext[level].at[pl.ds(z[1], z[2]), pl.ds(y[1], y[2]), :]
        else:
            face = 0 if dx == 1 else 1
            z, y = lv["pg"][dz], lv["py"][dy]
            src = pack[level].at[face, pl.ds(z[0], z[2]), pl.ds(y[0], y[2]), :]
            dst = halo[level].at[face, pl.ds(z[1], z[2]), pl.ds(y[1], y[2]), :]
        return src, dst

    for level in range(3):
        for step in STEPS:
            source, _ = neighbour(step, -1)
            _, dst = places(level, step)

            @pl.when(jnp.logical_not(source))
            def _():
                dst[...] = jnp.zeros(dst.shape, F32)

    def pack_faces(level):
        lv, src = LEVELS[level], ext[level]
        start, planes = lv["own"]
        lane = iota((lv["packrows"], 128), 1) // 8
        for g in range(lv["groups"]):
            faces = [jnp.zeros((lv["packrows"], 128), F32) for _ in range(2)]
            for j in range(min(16, planes - 16 * g)):
                parts = [src[start + 16 * g + j, r : r + n, :] for r, n in lv["tiles"]]
                v = parts[0] if len(parts) == 1 else jnp.concatenate(parts, axis=0)
                for f in range(2):
                    faces[f] = pick(lane == j, pltpu.roll(v, (8 * j - lv["face"][f]) % 128, 1), faces[f])
            for f in range(2):
                pack[level][f, g] = faces[f]

    def copies(level):
        result = []
        for index, step in enumerate(STEPS):
            target, device = neighbour(step, 1)
            source, _ = neighbour(step, -1)
            src, dst = places(level, step)
            copy = pltpu.make_async_remote_copy(
                src_ref=src, dst_ref=dst, send_sem=send_sem.at[level, index], recv_sem=recv_sem.at[level, index],
                device_id=device, device_id_type=MESH)
            result.append((target, source, copy))
        return result

    def send(level):
        for target, _, copy in copies(level):
            @pl.when(target)
            def _():
                copy.start()

    def receive(level):
        for _, source, copy in copies(level):
            @pl.when(source)
            def _():
                copy.wait_recv()

    def finish(level):
        for target, _, copy in copies(level):
            @pl.when(target)
            def _():
                copy.wait_send()

    def unpack(level, target):
        lv = LEVELS[level]
        rows = lv["keep"]
        lane = iota((rows, 128), 1)
        hi, lo = lv["lanes"]
        is_hi, is_lo = (lane >= hi) & (lane < hi + 8), (lane >= lo) & (lane < lo + 8)
        for first, count, g, j0 in lv["runs"]:
            for i in range(count):
                e, j = first + i, j0 + i
                low = pltpu.roll(halo[level][0, g], (lo - 8 * j) % 128, 1)
                high = pltpu.roll(halo[level][1, g], (hi - 8 * j) % 128, 1)
                own = 0.0 if level == 0 else ext[level][e, 0:rows, :]
                v = pick(is_hi, high, pick(is_lo, low, own))
                target[e] = pick(lane < 64, v, pltpu.roll(v, 64, 1)) if level == 2 else v

    load.wait()
    pack_faces(0)
    reach = [1 + jnp.minimum(g, 1) + jnp.minimum(n - 1 - g, 1) for g, n in ((gz, nz), (gy, ny), (gx, nx))]
    pl.semaphore_wait(barrier, reach[0] * reach[1] * reach[2] - 1)
    send(0)

    load_taps.wait()

    def tap_row(level, term):
        return [taps[level, term, k] for k in range(17)]

    def tap_pair(level, second):
        return [jnp.where(second, taps[level, 1, k], taps[level, 0, k]) for k in range(17)]

    def inside(coord, g, n, count):
        return (coord + g * n >= 0) & (coord + g * n < n * count)

    for t in range(2):
        high, low = split(band(x_coords(iota((256, 128), 0), 0) - iota((256, 128), 1), tap_row(0, t)))
        cols = slice(128 * t, 128 * (t + 1))
        x0[0:256, cols], x0[256:512, cols], x0[512:768, cols] = high, high, low
    m = iota((256, 128), 1) - 2
    high = pick((m < 67) & inside(m, gx, 64, nx), weight(x_coords(iota((256, 128), 0), 0) - 2 * m), 0.0).astype(BF16)
    xr1[0:256], xr1[256:512] = high, high
    c = iota((128, 128), 1) - 3
    high = pick((c < 36) & inside(c, gx, 32, nx), weight(x_coords(iota((128, 128), 0), 1) - 2 * c), 0.0).astype(BF16)
    xr2[0:128], xr2[128:256] = high, high
    sq = (128, 128)
    row, col = iota(sq, 0), iota(sq, 1)
    m_col, m_row, c_col, c_row = col - 1, row - 1, col - 2, row - 2
    up1 = pick(m_row < 66, weight(col - 2 * m_row), 0.0)
    up2 = pick((c_row < 35) & (m_col < 66) & inside(m_col, gx, 64, nx), weight(m_col - 2 * c_row), 0.0)
    up21 = exact(up2, up1)
    for t in range(2):
        k1 = pick((m_col < 66) & inside(m_col, gx, 64, nx), band(x_coords(row, 1) - m_col, tap_row(1, t)), 0.0)
        high, low = split(exact(k1, up1))
        for first, part in ((0, high), (256, high), (512, low)):
            x1[first + 128 * t : first + 128 * (t + 1)] = part
    k2 = band(x_coords(pick(row < 64, row, row - 64), 2) - c_col, tap_pair(2, row >= 64))
    k2 = pick((c_col < 35) & inside(c_col, gx, 32, nx), k2, 0.0)
    high, low = split(exact(k2, up21))
    x2[0:128], x2[128:256], x2[256:384] = high, high, low

    row, col = iota((32, 128), 0), iota((32, 128), 1)
    m = pick(row < 24, row - 2, row - 24 + 3)
    yr1[...] = pick((m < 19) & inside(m, gy, 16, ny), weight(y_coords(col, 0) - 2 * m), 0.0).astype(BF16)
    y0[0:32], y0[32:64] = split(band(y_coords(pick(col >= 48, col - 48, col), 0) - row, tap_pair(0, col >= 48)))
    m_col = col - 1
    yup1 = pick(m_col < 18, weight(row - 2 * m_col), 0.0)
    row, col = iota((24, 128), 0), iota((24, 128), 1)
    c = pick(row < 16, row - 3, row - 16 + 4)
    yr2[...] = pick((c < 12) & inside(c, gy, 8, ny), weight(y_coords(col, 1) - 2 * c), 0.0).astype(BF16)
    row, col = iota(sq, 0), iota(sq, 1)
    m_row, c_col, c_row = row - 1, col - 2, row - 2
    yup2 = pick((m_row < 18) & inside(m_row, gy, 16, ny) & (c_col < 11), weight(m_row - 2 * c_col), 0.0)
    yup21 = exact(yup1, yup2)
    for t in range(2):
        k1 = pick((m_row < 18) & inside(m_row, gy, 16, ny), band(y_coords(col, 1) - m_row, tap_row(1, t)), 0.0)
        y1[64 * t : 64 * t + 32], y1[64 * t + 32 : 64 * t + 64] = split(exact(yup1, k1))
        k2 = pick((c_row < 11) & inside(c_row, gy, 8, ny), band(y_coords(col, 2) - c_row, tap_row(2, t)), 0.0)
        y2[32 * t : 32 * t + 32], y2[64 + 32 * t : 96 + 32 * t] = split(exact(yup21, k2))

    z_low = jnp.where(gz > 0, 1.0, 0.0).astype(F32)
    z_high = jnp.where(gz < nz - 1, 1.0, 0.0).astype(F32)

    def edge(v, low, high):
        n = v.shape[0]
        return jnp.concatenate([v[:low] * z_low, v[low : n - high], v[n - high :] * z_high], axis=0)

    def join(parts, axis):
        return parts[0] if len(parts) == 1 else jnp.concatenate(parts, axis=axis)

    def pieces(v, count):
        return [v[:, 128 * i : 128 * (i + 1)] for i in range(count)]

    receive(0)
    unpack(0, side)

    def restrict_z(i, _):
        rows = pl.ds(pl.multiple_of(8 * i, 8), 8)

        def line(ref):
            even, odd = (jnp.concatenate([ref[2 * k + h : 2 * k + h + 1, rows, :] for k in range(24)], axis=0) for h in range(2))
            v = even[2:23] + 0.5625 * (odd[1:22] + odd[2:23]) - 0.0625 * (odd[0:21] + odd[3:24])
            return edge(v, 2, 3)

        r0[:, rows, 0:128] = line(e0)
        r0[:, rows, 128:256] = line(side)
        return 0

    lax.fori_loop(0, 6, restrict_z, 0)
    for p in range(0, 21, 7):
        high, low = split(join([r0[p + i, :, 0:128] for i in range(7)] + [r0[p + i, :, 128:256] for i in range(7)], 1))
        v = pieces(dot(yr1[:, 0:48], high) + dot(yr1[:, 0:48], low), 14)
        v = join([join([v[i], v[7 + i]], 1) for i in range(7)], 0)
        v = dot(join(split(v), 1), xr1[...]).reshape(7, 32, 128)
        for i in range(7):
            e1[7 + p + i, 8:32, :] = v[i, 0:24]
            e1[7 + p + i, 40:48, :] = v[i, 24:32]
    pack_faces(1)
    send(1)

    def conv_x0(i, _):
        planes = pl.ds(8 * i, 8)
        own_high, own_low = split(e0[planes].reshape(384, 128))
        side_high, side_low = split(side[planes].reshape(384, 128))
        left = join([own_high, side_high, own_low, side_low, own_high, side_high], 1)
        v = dot(left, x0[...])
        for t in range(2):
            f0[t, planes] = v[:, 128 * t : 128 * (t + 1)].reshape(8, 48, 128)
        return 0

    lax.fori_loop(0, 6, conv_x0, 0)

    def conv_z(field, row, count):
        total = row[0] * field(0, count)
        for k in range(1, 17):
            total = total + row[k] * field(k, count)
        return total

    def conv_z0(i, _):
        rows = pl.ds(pl.multiple_of(8 * i, 8), 8)
        for t in range(2):
            target = pl.ds(pl.multiple_of(48 * t + 8 * i, 8), 8)
            s0[:, target, :] = conv_z(lambda k, n: f0[t, k : k + n, rows, :], tap_row(0, t), 32)
        return 0

    lax.fori_loop(0, 6, conv_z0, 0)

    def fine_y(i, _):
        high, low = split(join([s0[4 * i + k] for k in range(4)], 1))
        both = dot(y0[:, 0:96], high)
        v = pieces(both[0:32] + both[32:64] + dot(y0[0:32, 0:96], low), 4)
        for k in range(4):
            out[2 * i + k // 2, k % 2] = v[k]
        return 0

    lax.fori_loop(0, 8, fine_y, 0)

    receive(1)
    unpack(1, v1)

    def restrict_z1(i, _):
        rows = pl.ds(pl.multiple_of(8 * i, 8), 8)
        even = jnp.concatenate([v1[2 * k : 2 * k + 1, rows, :] for k in range(18)], axis=0)
        odd = jnp.concatenate([v1[2 * k + 1 : 2 * k + 2, rows, :] for k in range(17)], axis=0)
        v = odd[1:16] + 0.5625 * (even[1:16] + even[2:17]) - 0.0625 * (even[0:15] + even[3:18])
        r1[:, rows, :] = edge(v, 3, 4)
        return 0

    lax.fori_loop(0, 5, restrict_z1, 0)
    high, low = split(join([r1[p] for p in range(15)], 1))
    v = dot(yr2[:, 0:40], high) + dot(yr2[:, 0:40], low)
    v = dot(join(split(join(pieces(v, 15), 0)), 1), xr2[...]).reshape(15, 24, 128)
    for p in range(15):
        e2[7 + p, 8:24, :] = v[p, 0:16]
        e2[7 + p, 32:40, :] = v[p, 16:24]
    pack_faces(2)
    send(2)

    def conv_z1(i, _):
        rows = pl.ds(pl.multiple_of(8 * i, 8), 8)
        for t in range(2):
            z1[t, :, rows, :] = edge(conv_z(lambda k, n: v1[k : k + n, rows, :], tap_row(1, t), 19), 1, 2)
        return 0

    lax.fori_loop(0, 5, conv_z1, 0)
    for t in range(2):
        for p, n in ((0, 7), (7, 6), (13, 6)):
            high, low = split(join([z1[t, p + i] for i in range(n)], 1))
            both = dot(y1[64 * t : 64 * t + 64, 0:40], high)
            v = both[0:32] + both[32:64] + dot(y1[64 * t : 64 * t + 32, 0:40], low)
            for i, piece in enumerate(pieces(v, n)):
                q1h[p + i, :, 128 * t : 128 * (t + 1)], q1l[p + i, :, 128 * t : 128 * (t + 1)] = split(piece)
    for p, n in ((0, 7), (7, 6), (13, 6)):
        high, low = (r[p : p + n].reshape(32 * n, 256) for r in (q1h, q1l))
        t1[p : p + n] = dot(join([high, low, high], 1), x1[...]).reshape(n, 32, 128)

    def refine(g, n):
        even = g[1 : n + 1]
        return even, 0.5625 * (even + g[2 : n + 2]) - 0.0625 * (g[0:n] + g[3 : n + 3])

    def add_middle(i, _):
        rows = pl.ds(pl.multiple_of(8 * i, 8), 8)
        for h, v in enumerate(refine(t1[:, rows, :], 16)):
            out[:, h, rows, :] = out[:, h, rows, :] + v
        return 0

    lax.fori_loop(0, 4, add_middle, 0)

    for level in range(3):
        finish(level)
    receive(2)
    unpack(2, v2)

    first_term = iota((8, 128), 1) < 64

    def conv_z2(i, _):
        rows = pl.ds(pl.multiple_of(8 * i, 8), 8)
        row = [v[None] for v in tap_pair(2, jnp.logical_not(first_term))]
        z2[:, rows, :] = edge(conv_z(lambda k, n: v2[k : k + n, rows, :], row, 13), 2, 3)
        return 0

    lax.fori_loop(0, 4, conv_z2, 0)
    lane = iota((32, 128), 1)
    for p, n in ((0, 7), (7, 6)):
        high, low = split(join([z2[p + i] for i in range(n)], 1))
        both, rest = dot(y2[:, 0:32], high), dot(y2[0:64, 0:32], low)
        terms = [pieces(both[32 * t : 32 * t + 32] + both[64 + 32 * t : 96 + 32 * t] + rest[32 * t : 32 * t + 32], n) for t in range(2)]
        high, low = split(join([pick(lane < 64, a, b) for a, b in zip(*terms)], 0))
        t2[p : p + n] = dot(join([high, low, high], 1), x2[...]).reshape(n, 32, 128)

    def add_coarse(i, _):
        rows = pl.ds(pl.multiple_of(8 * i, 8), 8)
        h = t2[:, rows, :]
        even = h[2:11]
        odd = 0.5625 * (h[1:11] + h[2:12]) - 0.0625 * (h[0:10] + h[3:13])
        g = []
        for k in range(9):
            g += [odd[k : k + 1], even[k : k + 1]]
        g = edge(jnp.concatenate(g + [odd[9:10]], axis=0), 1, 2)
        for h, v in enumerate(refine(g, 16)):
            out[:, h, rows, :] = out[:, h, rows, :] + v
        return 0

    lax.fori_loop(0, 4, add_coarse, 0)


def solution(mesh):
    counts = tuple(mesh.shape[a] for a in ("gz", "gy", "gx"))

    def local(charges, kernel_taps):
        vm = pltpu.VMEM
        scratch = [
            vm((48, 48, 128), F32), vm((35, 48, 128), F32), vm((29, 40, 128), F32),
            vm((2, 4, 48, 128), F32), vm((2, 4, 40, 128), F32), vm((2, 3, 32, 128), F32),
            vm((2, 2, 32, 128), F32), vm((2, 2, 32, 128), F32), vm((2, 1, 24, 128), F32),
            vm((48, 48, 128), F32), vm((35, 40, 128), F32), vm((29, 32, 128), F32),
            vm((21, 48, 256), F32), vm((15, 40, 128), F32), vm((2, 48, 48, 128), F32), vm((32, 96, 128), F32),
            vm((2, 19, 40, 128), F32), vm((19, 32, 256), BF16), vm((19, 32, 256), BF16), vm((19, 32, 128), F32),
            vm((13, 32, 128), F32), vm((13, 32, 128), F32),
            vm((768, 256), BF16), vm((512, 128), BF16), vm((768, 128), BF16), vm((256, 128), BF16), vm((384, 128), BF16),
            vm((32, 128), BF16), vm((24, 128), BF16), vm((64, 128), BF16), vm((128, 128), BF16), vm((128, 128), BF16),
            pltpu.SMEM((3, 2, 17), F32),
            pltpu.SemaphoreType.DMA, pltpu.SemaphoreType.DMA, pltpu.SemaphoreType.DMA((3, 26)), pltpu.SemaphoreType.DMA((3, 26)),
        ]
        result = pl.pallas_call(
            functools.partial(kernel, counts),
            out_shape=jax.ShapeDtypeStruct((16, 2, 32, 128), F32),
            in_specs=[pl.BlockSpec(memory_space=pltpu.HBM)] * 2,
            out_specs=pl.BlockSpec(memory_space=pltpu.VMEM),
            scratch_shapes=scratch,
            compiler_params=pltpu.CompilerParams(
                collective_id=0, has_side_effects=True, vmem_limit_bytes=26 * 1024 * 1024),
        )(*(pltpu.with_memory_space_constraint(a, pltpu.HBM) for a in (charges, kernel_taps)))
        return result.reshape(32, 32, 128)

    return jax.shard_map(
        local, mesh=mesh, in_specs=(P("gz", "gy", "gx"), P()), out_specs=P("gz", "gy", "gx"), check_vma=False)
```

time: 42.8 us -> 37 us (0.86)
  Pallas kernels: 40.7 us -> 36.1 us
  local copies, waits for them, and re-layouts: 1.87 us -> 0.8 us
    pallas_call x1, Pallas kernels: 40.7 us -> 36.1 us  [local(): pl.pallas_call(functools.partial(kernel, counts), out_shape=jax.ShapeDtyp...]
    unnamed x1, local copies, waits for them, and re-layouts: 1.87 us -> 0.8 us
where the time goes in v2:
time: 37 us; the launch traced here: 36.9 us
  Pallas kernels  36.1 us (98%)
  local copies, waits for them, and re-layouts  0.8 us (2%)
    pallas_call x1, Pallas kernels, local(): pl.pallas_call(functools.partial(kernel, counts), out_shape=jax.ShapeDtyp...  36.1 us
    unnamed x1, local copies, waits for them, and re-layouts  0.8 us

profile of v2, /device:TPU:7, one launch (start us, length us, event | category | flops | bytes accessed | tf_op | source)
XLA Modules:
  0.0 36.9 jit_solution(4882782754864478357)
XLA Ops:
  0.0 36.1 %shard_map.28 = f32[16,2,32,128]{3,2,1,0:T(8,128)S(1)} custom-call(f32[32,32,128]{2,1,0:T(8,128)} %q_hbm.1, f32[3,2,17]{2,1,0:T(2,128)} %taps_hbm.1), custom_call_target="tpu_custom_call" | custom-call | tf_op jit(solution)/shard_map/pallas_call | solution.py:445
  36.1 0.8 %copy.4 = f32[32,32,128]{2,1,0:T(8,128)} copy(f32[32,32,128]{2,1,0:T(8,128)S(1)} %bitcast.1) | data formatting | bytes 1048576

commit v3 on v2

--- a/solution.py
+++ b/solution.py
@@ -13,19 +13,27 @@
 
 LEVELS = (
     dict(keep=48, own=(8, 32), z={0: (8, 8, 32), 1: (32, 0, 8), -1: (8, 40, 8)},
-         y={0: (8, 8, 32), 1: (32, 0, 8), -1: (8, 40, 8)}, tiles=((8, 32),), packrows=32, groups=2, lanes=(80, 88),
+         y={0: (8, 8, 32), 1: (32, 0, 8), -1: (8, 40, 8)}, tiles=((8, 32),), packrows=32, groups=(0, 16), width=8,
          py={0: (0, 8, 32), 1: (24, 0, 8), -1: (0, 40, 8)}, pg={0: (0, 1, 2), 1: (1, 0, 1), -1: (0, 3, 1)},
-         face=(120, 0), runs=((0, 8, 0, 8), (8, 16, 1, 0), (24, 16, 2, 0), (40, 8, 3, 0))),
+         face=(120, 0), hi=(80, 8, 0), lo=(88, 8, 0), runs=((0, 8, 0, 8), (8, 16, 1, 0), (24, 16, 2, 0), (40, 8, 3, 0))),
     dict(keep=40, own=(7, 21), z={0: (7, 7, 21), 1: (16, 0, 7), -1: (12, 28, 7)},
-         y={0: (8, 8, 24), 1: (16, 0, 8), -1: (40, 32, 8)}, tiles=((8, 24), (40, 8)), packrows=32, groups=2, lanes=(80, 88),
-         py={0: (0, 8, 24), 1: (8, 0, 8), -1: (24, 32, 8)}, pg={0: (0, 1, 2), 1: (0, 0, 1), -1: (0, 3, 1)},
-         face=(56, 5), runs=((0, 7, 0, 9), (7, 16, 1, 0), (23, 5, 2, 0), (28, 7, 3, 5))),
-    dict(keep=32, own=(7, 15), z={0: (7, 7, 15), 1: (8, 0, 7), -1: (14, 22, 7)},
-         y={0: (8, 8, 16), 1: (8, 0, 8), -1: (32, 24, 8)}, tiles=((8, 16), (32, 8)), packrows=24, groups=1, lanes=(40, 48),
-         py={0: (0, 8, 16), 1: (0, 0, 8), -1: (16, 24, 8)}, pg={0: (0, 1, 1), 1: (0, 0, 1), -1: (0, 2, 1)},
-         face=(24, 7), runs=((0, 7, 0, 1), (7, 15, 1, 0), (22, 7, 2, 7))),
+         y={0: (8, 8, 24), 1: (16, 0, 8), -1: (40, 32, 8)}, tiles=((8, 24), (40, 8)), packrows=32, groups=(0, 8, 16, 4), width=16,
+         py={0: (0, 8, 24), 1: (8, 0, 8), -1: (24, 32, 8)}, pg={0: (0, 1, 3), 1: (1, 0, 1), -1: (3, 4, 1)},
+         face=(51, 0), hi=(80, 16, 0), lo=(96, 16, 0), runs=((0, 7, 0, 1), (7, 8, 1, 0), (15, 8, 2, 0), (23, 5, 3, 0), (28, 7, 4, 1))),
+    dict(keep=32, own=(7, 15), z={0: (3, 3, 6), 1: (4, 0, 3), -1: (6, 9, 3)},
+         y={0: (8, 8, 16), 1: (8, 0, 8), -1: (32, 24, 8)}, tiles=((8, 16), (32, 8)), packrows=24, groups=(0, 8, 7), width=16,
+         py={0: (0, 8, 16), 1: (0, 0, 8), -1: (16, 24, 8)}, pg={0: (0, 1, 2), 1: (0, 0, 1), -1: (2, 3, 1)},
+         face=(21, 0), hi=(37, 13, 0), lo=(50, 13, 3), runs=((0, 7, 0, 1), (7, 8, 1, 0), (15, 7, 2, 0), (22, 7, 3, 0))),
 )
 STEPS = tuple((dz, dy, dx) for dx in (1, -1, 0) for dy in (1, -1, 0) for dz in (1, -1, 0) if (dz, dy, dx) != (0, 0, 0))
+
+
+def coarse_place(e):
+    if e < 7:
+        return e // 3, 42 * (e % 3)
+    if e < 22:
+        return 3 + (e - 5) // 3, 42 * ((e - 5) % 3)
+    return 9 + (e - 22) // 3, 42 * ((e - 22) % 3)
 
 
 def split(x):
@@ -43,6 +51,10 @@
 
 def dot(a, b):
     return jnp.dot(a, b, preferred_element_type=F32)
+
+
+def join(parts, axis):
+    return parts[0] if len(parts) == 1 else jnp.concatenate(parts, axis=axis)
 
 
 def exact(a, b):
@@ -62,16 +74,12 @@
 
 
 def x_coords(slot, level):
-    if level == 0:
-        base, hi, lo, first, tile = 128, 128, -8, 0, 128
-    elif level == 1:
-        base, hi, lo, first, tile = 69, 67, -10, -2, 0
-    else:
-        base, hi, lo, first, tile = 39, 36, -11, -3, 0
+    base, first, high, low, tile = ((128, 0, 128, -8, 128), (67, -1, 63, -14, 0), (37, -2, 30, -10, 0))[level]
     coord = pick(slot < base, slot + first, NOWHERE)
-    h, l = slot - tile - LEVELS[level]["lanes"][0], slot - tile - LEVELS[level]["lanes"][1]
-    coord = pick((h >= 0) & (h < 8), h + hi, coord)
-    return pick((l >= 0) & (l < 8), l + lo, coord)
+    for (start, count, _), value in ((LEVELS[level]["hi"], high), (LEVELS[level]["lo"], low)):
+        k = slot - tile - start
+        coord = pick((k >= 0) & (k < count), k + value, coord)
+    return coord
 
 
 def y_coords(row, level):
@@ -138,61 +146,71 @@
                 dst[...] = jnp.zeros(dst.shape, F32)
 
     def pack_faces(level):
-        lv, src = LEVELS[level], ext[level]
+        lv, src, width = LEVELS[level], ext[level], LEVELS[level]["width"]
         start, planes = lv["own"]
-        lane = iota((lv["packrows"], 128), 1) // 8
-        for g in range(lv["groups"]):
+        lane = iota((lv["packrows"], 128), 1) // width
+        for g, offset in enumerate(lv["groups"]):
             faces = [jnp.zeros((lv["packrows"], 128), F32) for _ in range(2)]
-            for j in range(min(16, planes - 16 * g)):
-                parts = [src[start + 16 * g + j, r : r + n, :] for r, n in lv["tiles"]]
-                v = parts[0] if len(parts) == 1 else jnp.concatenate(parts, axis=0)
+            for j in range(min(128 // width, planes - offset)):
+                e, shift = start + offset + j, width * j
+                if level == 2:
+                    e, first = coarse_place(e)
+                    shift -= first
+                v = join([src[e, r : r + n, :] for r, n in lv["tiles"]], 0)
                 for f in range(2):
-                    faces[f] = pick(lane == j, pltpu.roll(v, (8 * j - lv["face"][f]) % 128, 1), faces[f])
+                    faces[f] = pick(lane == j, pltpu.roll(v, (shift - lv["face"][f]) % 128, 1), faces[f])
             for f in range(2):
                 pack[level][f, g] = faces[f]
 
-    def copies(level):
+    def copies(level, across):
         result = []
         for index, step in enumerate(STEPS):
+            if across is not None and (step[2] != 0) != across:
+                continue
             target, device = neighbour(step, 1)
             source, _ = neighbour(step, -1)
             src, dst = places(level, step)
             copy = pltpu.make_async_remote_copy(
-                src_ref=src, dst_ref=dst, send_sem=send_sem.at[level, index], recv_sem=recv_sem.at[level, index],
+                src_ref=src, dst_ref=dst, send_sem=send_sem.at[level % 2, index], recv_sem=recv_sem.at[level, index],
                 device_id=device, device_id_type=MESH)
             result.append((target, source, copy))
         return result
 
-    def send(level):
-        for target, _, copy in copies(level):
+    def send(level, across):
+        for target, _, copy in copies(level, across):
             @pl.when(target)
             def _():
                 copy.start()
 
-    def receive(level):
-        for _, source, copy in copies(level):
+    def receive(level, across):
+        for _, source, copy in copies(level, across):
             @pl.when(source)
             def _():
                 copy.wait_recv()
 
     def finish(level):
-        for target, _, copy in copies(level):
+        for target, _, copy in copies(level, None):
             @pl.when(target)
             def _():
                 copy.wait_send()
 
     def unpack(level, target):
         lv = LEVELS[level]
-        rows = lv["keep"]
+        rows, width = lv["keep"], lv["width"]
         lane = iota((rows, 128), 1)
-        hi, lo = lv["lanes"]
-        is_hi, is_lo = (lane >= hi) & (lane < hi + 8), (lane >= lo) & (lane < lo + 8)
+        (hi, hi_count, hi_skip), (lo, lo_count, lo_skip) = lv["hi"], lv["lo"]
+        is_hi, is_lo = (lane >= hi) & (lane < hi + hi_count), (lane >= lo) & (lane < lo + lo_count)
         for first, count, g, j0 in lv["runs"]:
             for i in range(count):
-                e, j = first + i, j0 + i
-                low = pltpu.roll(halo[level][0, g], (lo - 8 * j) % 128, 1)
-                high = pltpu.roll(halo[level][1, g], (hi - 8 * j) % 128, 1)
-                own = 0.0 if level == 0 else ext[level][e, 0:rows, :]
+                e, j = first + i, width * (j0 + i)
+                low = pltpu.roll(halo[level][0, g], (lo - lo_skip - j) % 128, 1)
+                high = pltpu.roll(halo[level][1, g], (hi - hi_skip - j) % 128, 1)
+                if level == 2:
+                    place, shift = coarse_place(e)
+                    own = ext[level][place, 0:rows, :]
+                    own = pltpu.roll(own, 128 - shift, 1) if shift else own
+                else:
+                    own = 0.0 if level == 0 else ext[level][e, 0:rows, :]
                 v = pick(is_hi, high, pick(is_lo, low, own))
                 target[e] = pick(lane < 64, v, pltpu.roll(v, 64, 1)) if level == 2 else v
 
@@ -200,7 +218,8 @@
     pack_faces(0)
     reach = [1 + jnp.minimum(g, 1) + jnp.minimum(n - 1 - g, 1) for g, n in ((gz, nz), (gy, ny), (gx, nx))]
     pl.semaphore_wait(barrier, reach[0] * reach[1] * reach[2] - 1)
-    send(0)
+    send(0, False)
+    send(0, True)
 
     load_taps.wait()
 
@@ -217,14 +236,13 @@
         high, low = split(band(x_coords(iota((256, 128), 0), 0) - iota((256, 128), 1), tap_row(0, t)))
         cols = slice(128 * t, 128 * (t + 1))
         x0[0:256, cols], x0[256:512, cols], x0[512:768, cols] = high, high, low
-    m = iota((256, 128), 1) - 2
-    high = pick((m < 67) & inside(m, gx, 64, nx), weight(x_coords(iota((256, 128), 0), 0) - 2 * m), 0.0).astype(BF16)
-    xr1[0:256], xr1[256:512] = high, high
-    c = iota((128, 128), 1) - 3
-    high = pick((c < 36) & inside(c, gx, 32, nx), weight(x_coords(iota((128, 128), 0), 1) - 2 * c), 0.0).astype(BF16)
-    xr2[0:128], xr2[128:256] = high, high
     sq = (128, 128)
     row, col = iota(sq, 0), iota(sq, 1)
+    m, c = col - 1, col - 2
+    high = pick((m < 66) & inside(m, gx, 64, nx), weight(row - 2 * m), 0.0).astype(BF16)
+    xr1[0:128], xr1[128:256] = high, high
+    high = pick((row < 67) & (c < 35) & inside(c, gx, 32, nx), weight(row - 1 - 2 * c), 0.0).astype(BF16)
+    xr2[0:128], xr2[128:256] = high, high
     m_col, m_row, c_col, c_row = col - 1, row - 1, col - 2, row - 2
     up1 = pick(m_row < 66, weight(col - 2 * m_row), 0.0)
     up2 = pick((c_row < 35) & (m_col < 66) & inside(m_col, gx, 64, nx), weight(m_col - 2 * c_row), 0.0)
@@ -242,7 +260,8 @@
     row, col = iota((32, 128), 0), iota((32, 128), 1)
     m = pick(row < 24, row - 2, row - 24 + 3)
     yr1[...] = pick((m < 19) & inside(m, gy, 16, ny), weight(y_coords(col, 0) - 2 * m), 0.0).astype(BF16)
-    y0[0:32], y0[32:64] = split(band(y_coords(pick(col >= 48, col - 48, col), 0) - row, tap_pair(0, col >= 48)))
+    for t in range(2):
+        y0[64 * t : 64 * t + 32], y0[64 * t + 32 : 64 * t + 64] = split(band(y_coords(col, 0) - row, tap_row(0, t)))
     m_col = col - 1
     yup1 = pick(m_col < 18, weight(row - 2 * m_col), 0.0)
     row, col = iota((24, 128), 0), iota((24, 128), 1)
@@ -265,50 +284,84 @@
         n = v.shape[0]
         return jnp.concatenate([v[:low] * z_low, v[low : n - high], v[n - high :] * z_high], axis=0)
 
-    def join(parts, axis):
-        return parts[0] if len(parts) == 1 else jnp.concatenate(parts, axis=axis)
-
     def pieces(v, count):
         return [v[:, 128 * i : 128 * (i + 1)] for i in range(count)]
 
-    receive(0)
-    unpack(0, side)
+    receive(0, False)
 
     def restrict_z(i, _):
         rows = pl.ds(pl.multiple_of(8 * i, 8), 8)
-
-        def line(ref):
-            even, odd = (jnp.concatenate([ref[2 * k + h : 2 * k + h + 1, rows, :] for k in range(24)], axis=0) for h in range(2))
-            v = even[2:23] + 0.5625 * (odd[1:22] + odd[2:23]) - 0.0625 * (odd[0:21] + odd[3:24])
-            return edge(v, 2, 3)
-
-        r0[:, rows, 0:128] = line(e0)
-        r0[:, rows, 128:256] = line(side)
+        even, odd = (jnp.concatenate([e0[2 * k + h : 2 * k + h + 1, rows, :] for k in range(24)], axis=0) for h in range(2))
+        v = even[2:23] + 0.5625 * (odd[1:22] + odd[2:23]) - 0.0625 * (odd[0:21] + odd[3:24])
+        r0[:, rows, :] = edge(v, 2, 3)
         return 0
 
     lax.fori_loop(0, 6, restrict_z, 0)
     for p in range(0, 21, 7):
-        high, low = split(join([r0[p + i, :, 0:128] for i in range(7)] + [r0[p + i, :, 128:256] for i in range(7)], 1))
-        v = pieces(dot(yr1[:, 0:48], high) + dot(yr1[:, 0:48], low), 14)
-        v = join([join([v[i], v[7 + i]], 1) for i in range(7)], 0)
+        high, low = split(join([r0[p + i] for i in range(7)], 1))
+        v = join(pieces(dot(yr1[:, 0:48], high) + dot(yr1[:, 0:48], low), 7), 0)
         v = dot(join(split(v), 1), xr1[...]).reshape(7, 32, 128)
         for i in range(7):
             e1[7 + p + i, 8:32, :] = v[i, 0:24]
             e1[7 + p + i, 40:48, :] = v[i, 24:32]
+    send(1, False)
     pack_faces(1)
-    send(1)
+    send(1, True)
+    receive(0, True)
+    unpack(0, side)
 
     def conv_x0(i, _):
-        planes = pl.ds(8 * i, 8)
-        own_high, own_low = split(e0[planes].reshape(384, 128))
-        side_high, side_low = split(side[planes].reshape(384, 128))
+        planes = pl.ds(16 * i, 16)
+        own_high, own_low = split(e0[planes].reshape(768, 128))
+        side_high, side_low = split(side[planes].reshape(768, 128))
         left = join([own_high, side_high, own_low, side_low, own_high, side_high], 1)
         v = dot(left, x0[...])
         for t in range(2):
-            f0[t, planes] = v[:, 128 * t : 128 * (t + 1)].reshape(8, 48, 128)
-        return 0
-
-    lax.fori_loop(0, 6, conv_x0, 0)
+            f0[t, planes] = v[:, 128 * t : 128 * (t + 1)].reshape(16, 48, 128)
+        return 0
+
+    lax.fori_loop(0, 3, conv_x0, 0)
+
+    finish(0)
+    receive(1, False)
+
+    def restrict_z1(i, _):
+        rows = pl.ds(pl.multiple_of(8 * i, 8), 8)
+        even = jnp.concatenate([e1[2 * k : 2 * k + 1, rows, :] for k in range(18)], axis=0)
+        odd = jnp.concatenate([e1[2 * k + 1 : 2 * k + 2, rows, :] for k in range(17)], axis=0)
+        v = odd[1:16] + 0.5625 * (even[1:16] + even[2:17]) - 0.0625 * (even[0:15] + even[3:18])
+        r1[:, rows, :] = edge(v, 3, 4)
+        return 0
+
+    lax.fori_loop(0, 5, restrict_z1, 0)
+    high, low = split(join([r1[p] for p in range(15)], 1))
+    v = dot(yr2[:, 0:40], high) + dot(yr2[:, 0:40], low)
+    v = dot(join(split(join(pieces(v, 15), 0)), 1), xr2[...]).reshape(15, 24, 128)
+    for g in range(6):
+        w = None
+        for k in range(3):
+            p = 3 * g - 2 + k
+            if 0 <= p < 15:
+                part = pltpu.roll(v[p], 42 * k, 1) if k else v[p]
+                w = part if w is None else w + part
+        e2[3 + g, 8:24, :] = w[0:16]
+        e2[3 + g, 32:40, :] = w[16:24]
+    pack_faces(2)
+    send(2, True)
+    send(2, False)
+
+    def fine_y(i, _):
+        for t in range(2):
+            high, low = split(join([f0[t, 6 * i + k] for k in range(6)], 1))
+            matrix = y0[64 * t : 64 * t + 64, 0:48]
+            both = dot(matrix, high)
+            v = pieces(both[0:32] + both[32:64] + dot(matrix[0:32], low), 6)
+            for k in range(6):
+                s0[t, 6 * i + k] = v[k]
+        return 0
+
+    lax.fori_loop(0, 8, fine_y, 0)
+
 
     def conv_z(field, row, count):
         total = row[0] * field(0, count)
@@ -318,43 +371,16 @@
 
     def conv_z0(i, _):
         rows = pl.ds(pl.multiple_of(8 * i, 8), 8)
-        for t in range(2):
-            target = pl.ds(pl.multiple_of(48 * t + 8 * i, 8), 8)
-            s0[:, target, :] = conv_z(lambda k, n: f0[t, k : k + n, rows, :], tap_row(0, t), 32)
-        return 0
-
-    lax.fori_loop(0, 6, conv_z0, 0)
-
-    def fine_y(i, _):
-        high, low = split(join([s0[4 * i + k] for k in range(4)], 1))
-        both = dot(y0[:, 0:96], high)
-        v = pieces(both[0:32] + both[32:64] + dot(y0[0:32, 0:96], low), 4)
-        for k in range(4):
-            out[2 * i + k // 2, k % 2] = v[k]
-        return 0
-
-    lax.fori_loop(0, 8, fine_y, 0)
-
-    receive(1)
+        v = conv_z(lambda k, n: s0[0, k : k + n, rows, :], tap_row(0, 0), 32)
+        v = v + conv_z(lambda k, n: s0[1, k : k + n, rows, :], tap_row(0, 1), 32)
+        for k in range(32):
+            out[k // 2, k % 2, rows, :] = v[k]
+        return 0
+
+    lax.fori_loop(0, 4, conv_z0, 0)
+
+    receive(1, True)
     unpack(1, v1)
-
-    def restrict_z1(i, _):
-        rows = pl.ds(pl.multiple_of(8 * i, 8), 8)
-        even = jnp.concatenate([v1[2 * k : 2 * k + 1, rows, :] for k in range(18)], axis=0)
-        odd = jnp.concatenate([v1[2 * k + 1 : 2 * k + 2, rows, :] for k in range(17)], axis=0)
-        v = odd[1:16] + 0.5625 * (even[1:16] + even[2:17]) - 0.0625 * (even[0:15] + even[3:18])
-        r1[:, rows, :] = edge(v, 3, 4)
-        return 0
-
-    lax.fori_loop(0, 5, restrict_z1, 0)
-    high, low = split(join([r1[p] for p in range(15)], 1))
-    v = dot(yr2[:, 0:40], high) + dot(yr2[:, 0:40], low)
-    v = dot(join(split(join(pieces(v, 15), 0)), 1), xr2[...]).reshape(15, 24, 128)
-    for p in range(15):
-        e2[7 + p, 8:24, :] = v[p, 0:16]
-        e2[7 + p, 32:40, :] = v[p, 16:24]
-    pack_faces(2)
-    send(2)
 
     def conv_z1(i, _):
         rows = pl.ds(pl.multiple_of(8 * i, 8), 8)
@@ -386,9 +412,9 @@
 
     lax.fori_loop(0, 4, add_middle, 0)
 
-    for level in range(3):
-        finish(level)
-    receive(2)
+    finish(1)
+    finish(2)
+    receive(2, None)
     unpack(2, v2)
 
     first_term = iota((8, 128), 1) < 64
@@ -430,17 +456,17 @@
     def local(charges, kernel_taps):
         vm = pltpu.VMEM
         scratch = [
-            vm((48, 48, 128), F32), vm((35, 48, 128), F32), vm((29, 40, 128), F32),
-            vm((2, 4, 48, 128), F32), vm((2, 4, 40, 128), F32), vm((2, 3, 32, 128), F32),
-            vm((2, 2, 32, 128), F32), vm((2, 2, 32, 128), F32), vm((2, 1, 24, 128), F32),
+            vm((48, 48, 128), F32), vm((35, 48, 128), F32), vm((12, 40, 128), F32),
+            vm((2, 4, 48, 128), F32), vm((2, 5, 40, 128), F32), vm((2, 4, 32, 128), F32),
+            vm((2, 2, 32, 128), F32), vm((2, 4, 32, 128), F32), vm((2, 3, 24, 128), F32),
             vm((48, 48, 128), F32), vm((35, 40, 128), F32), vm((29, 32, 128), F32),
-            vm((21, 48, 256), F32), vm((15, 40, 128), F32), vm((2, 48, 48, 128), F32), vm((32, 96, 128), F32),
+            vm((21, 48, 128), F32), vm((15, 40, 128), F32), vm((2, 48, 48, 128), F32), vm((2, 48, 32, 128), F32),
             vm((2, 19, 40, 128), F32), vm((19, 32, 256), BF16), vm((19, 32, 256), BF16), vm((19, 32, 128), F32),
             vm((13, 32, 128), F32), vm((13, 32, 128), F32),
-            vm((768, 256), BF16), vm((512, 128), BF16), vm((768, 128), BF16), vm((256, 128), BF16), vm((384, 128), BF16),
-            vm((32, 128), BF16), vm((24, 128), BF16), vm((64, 128), BF16), vm((128, 128), BF16), vm((128, 128), BF16),
+            vm((768, 256), BF16), vm((256, 128), BF16), vm((768, 128), BF16), vm((256, 128), BF16), vm((384, 128), BF16),
+            vm((32, 128), BF16), vm((24, 128), BF16), vm((128, 128), BF16), vm((128, 128), BF16), vm((128, 128), BF16),
             pltpu.SMEM((3, 2, 17), F32),
-            pltpu.SemaphoreType.DMA, pltpu.SemaphoreType.DMA, pltpu.SemaphoreType.DMA((3, 26)), pltpu.SemaphoreType.DMA((3, 26)),
+            pltpu.SemaphoreType.DMA, pltpu.SemaphoreType.DMA, pltpu.SemaphoreType.DMA((2, 26)), pltpu.SemaphoreType.DMA((3, 26)),
         ]
         result = pl.pallas_call(
             functools.partial(kernel, counts),

time: 37 us -> 33.2 us (0.90)
  Pallas kernels: 36.1 us -> 32.3 us
    pallas_call x1, Pallas kernels: 36.1 us -> 32.3 us  [local(): pl.pallas_call(functools.partial(kernel, counts), out_shape=jax.ShapeDtyp...]
where the time goes in v3:
time: 33.2 us; the launch traced here: 33.1 us
  Pallas kernels  32.3 us (97%)
  local copies, waits for them, and re-layouts  0.8 us (2%)
    pallas_call x1, Pallas kernels, local(): pl.pallas_call(functools.partial(kernel, counts), out_shape=jax.ShapeDtyp...  32.3 us
    unnamed x1, local copies, waits for them, and re-layouts  0.8 us

profile of v3, /device:TPU:7, one launch (start us, length us, event | category | flops | bytes accessed | tf_op | source)
XLA Modules:
  0.0 33.1 jit_solution(10721690996057282322)
XLA Ops:
  0.0 32.3 %shard_map.28 = f32[16,2,32,128]{3,2,1,0:T(8,128)S(1)} custom-call(f32[32,32,128]{2,1,0:T(8,128)} %q_hbm.1, f32[3,2,17]{2,1,0:T(2,128)} %taps_hbm.1), custom_call_target="tpu_custom_call" | custom-call | tf_op jit(solution)/shard_map/pallas_call | solution.py:471
  32.3 0.8 %copy.4 = f32[32,32,128]{2,1,0:T(8,128)} copy(f32[32,32,128]{2,1,0:T(8,128)S(1)} %bitcast.1) | data formatting | bytes 1048576

commit v4 on v3

--- a/solution.py
+++ b/solution.py
@@ -1,4 +1,5 @@
 import functools
+import math
 
 import jax
 import jax.numpy as jnp
@@ -94,7 +95,7 @@
 
 def kernel(counts, q_hbm, taps_hbm, out, *scratch):
     (e0, e1, e2, px0, px1, px2, pk0, pk1, pk2, side, v1, v2, r0, r1, f0, s0, z1, q1h, q1l, t1, z2, t2,
-     x0, xr1, x1, xr2, x2, yr1, yr2, y0, y1, y2, taps, local_sem, taps_sem, send_sem, recv_sem) = scratch
+     x0, xr1, x1, xr2, x2, yr1, yr2, y0, y1, y2, taps, local_sem, taps_sem, measure, send_sem, recv_sem) = scratch
     ext, halo, pack = (e0, e1, e2), (px0, px1, px2), (pk0, pk1, pk2)
     nz, ny, nx = counts
     gz, gy, gx = lax.axis_index("gz"), lax.axis_index("gy"), lax.axis_index("gx")
@@ -164,35 +165,46 @@
 
     def copies(level, across):
         result = []
-        for index, step in enumerate(STEPS):
+        for step in STEPS:
             if across is not None and (step[2] != 0) != across:
                 continue
             target, device = neighbour(step, 1)
-            source, _ = neighbour(step, -1)
             src, dst = places(level, step)
             copy = pltpu.make_async_remote_copy(
-                src_ref=src, dst_ref=dst, send_sem=send_sem.at[level % 2, index], recv_sem=recv_sem.at[level, index],
+                src_ref=src, dst_ref=dst, send_sem=send_sem.at[level, step[2] % 3], recv_sem=recv_sem.at[level, step[2] % 3],
                 device_id=device, device_id_type=MESH)
-            result.append((target, source, copy))
+            result.append((target, copy))
         return result
 
     def send(level, across):
-        for target, _, copy in copies(level, across):
+        for target, copy in copies(level, across):
             @pl.when(target)
             def _():
                 copy.start()
 
+    def wait_all(level, semaphores, sign, kinds):
+        places_z = (gz == 0, (gz > 0) & (gz < nz - 1), gz == nz - 1)
+        places_y = (gy == 0, (gy > 0) & (gy < ny - 1), gy == ny - 1)
+        for dx in kinds:
+            side = {0: gx >= 0, 1: gx < nx - 1, -1: gx > 0}[sign * dx]
+            for z, at_z in enumerate(places_z):
+                for y, at_y in enumerate(places_y):
+                    units = 0
+                    for step in STEPS:
+                        if step[2] == dx and 0 <= z + sign * step[0] <= 2 and 0 <= y + sign * step[1] <= 2:
+                            shape = places(level, step)[1].shape
+                            units += math.prod(shape) // 1024
+                    whole = measure.at[pl.ds(0, units)]
+
+                    @pl.when(at_z & at_y & side)
+                    def _():
+                        pltpu.make_async_copy(whole, whole, semaphores.at[level, dx % 3]).wait()
+
     def receive(level, across):
-        for _, source, copy in copies(level, across):
-            @pl.when(source)
-            def _():
-                copy.wait_recv()
+        wait_all(level, recv_sem, -1, {None: (0, 1, -1), False: (0,), True: (1, -1)}[across])
 
     def finish(level):
-        for target, _, copy in copies(level, None):
-            @pl.when(target)
-            def _():
-                copy.wait_send()
+        wait_all(level, send_sem, 1, (0, 1, -1))
 
     def unpack(level, target):
         lv = LEVELS[level]
@@ -466,7 +478,7 @@
             vm((768, 256), BF16), vm((256, 128), BF16), vm((768, 128), BF16), vm((256, 128), BF16), vm((384, 128), BF16),
             vm((32, 128), BF16), vm((24, 128), BF16), vm((128, 128), BF16), vm((128, 128), BF16), vm((128, 128), BF16),
             pltpu.SMEM((3, 2, 17), F32),
-            pltpu.SemaphoreType.DMA, pltpu.SemaphoreType.DMA, pltpu.SemaphoreType.DMA((2, 26)), pltpu.SemaphoreType.DMA((3, 26)),
+            pltpu.SemaphoreType.DMA, pltpu.SemaphoreType.DMA, vm((160, 8, 128), F32), pltpu.SemaphoreType.DMA((3, 3)), pltpu.SemaphoreType.DMA((3, 3)),
         ]
         result = pl.pallas_call(
             functools.partial(kernel, counts),

time: 33.2 us -> 32.1 us (0.967)
  Pallas kernels: 32.3 us -> 31.2 us
    pallas_call x1, Pallas kernels: 32.3 us -> 31.2 us  [local(): pl.pallas_call(functools.partial(kernel, counts), out_shape=jax.ShapeDtyp...]
where the time goes in v4:
time: 32.1 us; the launch traced here: 32 us
  Pallas kernels  31.2 us (97%)
  local copies, waits for them, and re-layouts  0.8 us (2%)
    pallas_call x1, Pallas kernels, local(): pl.pallas_call(functools.partial(kernel, counts), out_shape=jax.ShapeDtyp...  31.2 us
    unnamed x1, local copies, waits for them, and re-layouts  0.8 us

profile of v4, /device:TPU:7, one launch (start us, length us, event | category | flops | bytes accessed | tf_op | source)
XLA Modules:
  0.0 32.0 jit_solution(5203025514138450171)
XLA Ops:
  0.0 31.2 %shard_map.28 = f32[16,2,32,128]{3,2,1,0:T(8,128)S(1)} custom-call(f32[32,32,128]{2,1,0:T(8,128)} %q_hbm.1, f32[3,2,17]{2,1,0:T(2,128)} %taps_hbm.1), custom_call_target="tpu_custom_call" | custom-call | tf_op jit(solution)/shard_map/pallas_call | solution.py:483
  31.2 0.8 %copy.4 = f32[32,32,128]{2,1,0:T(8,128)} copy(f32[32,32,128]{2,1,0:T(8,128)S(1)} %bitcast.1) | data formatting | bytes 1048576

commit v5 on v4

--- a/solution.py
+++ b/solution.py
@@ -24,7 +24,7 @@
     dict(keep=32, own=(7, 15), z={0: (3, 3, 6), 1: (4, 0, 3), -1: (6, 9, 3)},
          y={0: (8, 8, 16), 1: (8, 0, 8), -1: (32, 24, 8)}, tiles=((8, 16), (32, 8)), packrows=24, groups=(0, 8, 7), width=16,
          py={0: (0, 8, 16), 1: (0, 0, 8), -1: (16, 24, 8)}, pg={0: (0, 1, 2), 1: (0, 0, 1), -1: (2, 3, 1)},
-         face=(21, 0), hi=(37, 13, 0), lo=(50, 13, 3), runs=((0, 7, 0, 1), (7, 8, 1, 0), (15, 7, 2, 0), (22, 7, 3, 0))),
+         face=(21, 0), hi=(50, 13, 0), lo=(37, 13, 3), runs=((0, 7, 0, 1), (7, 8, 1, 0), (15, 7, 2, 0), (22, 7, 3, 0))),
 )
 STEPS = tuple((dz, dy, dx) for dx in (1, -1, 0) for dy in (1, -1, 0) for dz in (1, -1, 0) if (dz, dy, dx) != (0, 0, 0))
 
@@ -206,25 +206,35 @@
     def finish(level):
         wait_all(level, send_sem, 1, (0, 1, -1))
 
+    def unpack_own(target):
+        lane = iota((32, 128), 1)
+        for first, count, _, _ in LEVELS[2]["runs"]:
+            for e in range(first, first + count):
+                place, shift = coarse_place(e)
+                v = e2[place, 0:32, :]
+                v = pltpu.roll(v, 128 - shift, 1) if shift else v
+                target[e] = pick(lane < 64, v, pltpu.roll(v, 64, 1))
+
     def unpack(level, target):
         lv = LEVELS[level]
         rows, width = lv["keep"], lv["width"]
         lane = iota((rows, 128), 1)
-        (hi, hi_count, hi_skip), (lo, lo_count, lo_skip) = lv["hi"], lv["lo"]
-        is_hi, is_lo = (lane >= hi) & (lane < hi + hi_count), (lane >= lo) & (lane < lo + lo_count)
+        start = 34 if level == 2 else lv["hi"][0]
+        here = lane % 64 if level == 2 else lane
+        used = (here >= 37) & (here < 63) if level == 2 else (lane >= start) & (lane < start + 2 * width)
+        even = (lane // width) % 2 == 0
         for first, count, g, j0 in lv["runs"]:
+            leading, trailing = (halo[level][0, g], halo[level][1, g]) if level == 2 else (halo[level][1, g], halo[level][0, g])
+            trailing = pltpu.roll(trailing, width, 1)
+            pair = (pick(even, leading, trailing), pick(even, trailing, leading))
+            places = range(8) if level == 2 else range(j0, j0 + count)
+            moved = {j: pltpu.roll(pair[j % 2], (start - width * j) % 128, 1) for j in places}
             for i in range(count):
-                e, j = first + i, width * (j0 + i)
-                low = pltpu.roll(halo[level][0, g], (lo - lo_skip - j) % 128, 1)
-                high = pltpu.roll(halo[level][1, g], (hi - hi_skip - j) % 128, 1)
+                e, j = first + i, j0 + i
                 if level == 2:
-                    place, shift = coarse_place(e)
-                    own = ext[level][place, 0:rows, :]
-                    own = pltpu.roll(own, 128 - shift, 1) if shift else own
+                    target[e] = pick(used, pick(lane < 64, moved[j], moved[(j + 4) % 8]), target[e])
                 else:
-                    own = 0.0 if level == 0 else ext[level][e, 0:rows, :]
-                v = pick(is_hi, high, pick(is_lo, low, own))
-                target[e] = pick(lane < 64, v, pltpu.roll(v, 64, 1)) if level == 2 else v
+                    target[e] = pick(used, moved[j], 0.0 if level == 0 else ext[level][e, 0:rows, :])
 
     load.wait()
     pack_faces(0)
@@ -426,7 +436,9 @@
 
     finish(1)
     finish(2)
-    receive(2, None)
+    receive(2, False)
+    unpack_own(v2)
+    receive(2, True)
     unpack(2, v2)
 
     first_term = iota((8, 128), 1) < 64

time: 32.1 us -> 30.6 us (0.953)
  Pallas kernels: 31.2 us -> 29.7 us
    pallas_call x1, Pallas kernels: 31.2 us -> 29.7 us  [local(): pl.pallas_call(functools.partial(kernel, counts), out_shape=jax.ShapeDtyp...]
where the time goes in v5:
time: 30.6 us; the launch traced here: 30.5 us
  Pallas kernels  29.7 us (97%)
  local copies, waits for them, and re-layouts  0.8 us (3%)
    pallas_call x1, Pallas kernels, local(): pl.pallas_call(functools.partial(kernel, counts), out_shape=jax.ShapeDtyp...  29.7 us
    unnamed x1, local copies, waits for them, and re-layouts  0.8 us

profile of v5, /device:TPU:7, one launch (start us, length us, event | category | flops | bytes accessed | tf_op | source)
XLA Modules:
  0.0 30.5 jit_solution(8139011553317659503)
XLA Ops:
  0.0 29.7 %shard_map.28 = f32[16,2,32,128]{3,2,1,0:T(8,128)S(1)} custom-call(f32[32,32,128]{2,1,0:T(8,128)} %q_hbm.1, f32[3,2,17]{2,1,0:T(2,128)} %taps_hbm.1), custom_call_target="tpu_custom_call" | custom-call | tf_op jit(solution)/shard_map/pallas_call | solution.py:495
  29.7 0.8 %copy.4 = f32[32,32,128]{2,1,0:T(8,128)} copy(f32[32,32,128]{2,1,0:T(8,128)S(1)} %bitcast.1) | data formatting | bytes 1048576

commit v6 on v5

--- a/solution.py
+++ b/solution.py
@@ -153,13 +153,13 @@
         for g, offset in enumerate(lv["groups"]):
             faces = [jnp.zeros((lv["packrows"], 128), F32) for _ in range(2)]
             for j in range(min(128 // width, planes - offset)):
-                e, shift = start + offset + j, width * j
-                if level == 2:
-                    e, first = coarse_place(e)
-                    shift -= first
-                v = join([src[e, r : r + n, :] for r, n in lv["tiles"]], 0)
+                v = join([src[start + offset + j, r : r + n, :] for r, n in lv["tiles"]], 0)
                 for f in range(2):
-                    faces[f] = pick(lane == j, pltpu.roll(v, (shift - lv["face"][f]) % 128, 1), faces[f])
+                    if level == 0:
+                        faces[f] = pick(lane == j, pltpu.roll(v, (width * j - lv["face"][f]) % 128, 1), faces[f])
+                if level == 1:
+                    moved = pltpu.roll(v, (16 * j - 80) % 128, 1)
+                    faces = [pick(lane == (j + 1 - f) % 8, moved, faces[f]) for f in range(2)]
             for f in range(2):
                 pack[level][f, g] = faces[f]
 
@@ -225,7 +225,7 @@
         even = (lane // width) % 2 == 0
         for first, count, g, j0 in lv["runs"]:
             leading, trailing = (halo[level][0, g], halo[level][1, g]) if level == 2 else (halo[level][1, g], halo[level][0, g])
-            trailing = pltpu.roll(trailing, width, 1)
+            trailing = trailing if level else pltpu.roll(trailing, width, 1)
             pair = (pick(even, leading, trailing), pick(even, trailing, leading))
             places = range(8) if level == 2 else range(j0, j0 + count)
             moved = {j: pltpu.roll(pair[j % 2], (start - width * j) % 128, 1) for j in places}
@@ -261,9 +261,11 @@
     sq = (128, 128)
     row, col = iota(sq, 0), iota(sq, 1)
     m, c = col - 1, col - 2
-    high = pick((m < 66) & inside(m, gx, 64, nx), weight(row - 2 * m), 0.0).astype(BF16)
+    m = pick(col < 67, m, pick((col >= 80) & (col < 96), col - 81, pick((col >= 96) & (col < 112), col - 46, NOWHERE)))
+    high = pick(inside(m, gx, 64, nx), weight(row - 2 * m), 0.0).astype(BF16)
     xr1[0:128], xr1[128:256] = high, high
-    high = pick((row < 67) & (c < 35) & inside(c, gx, 32, nx), weight(row - 1 - 2 * c), 0.0).astype(BF16)
+    c = pick(col < 37, c, pick((col >= 48) & (col < 64), col - 29, pick((col >= 64) & (col < 80), col - 66, NOWHERE)))
+    high = pick((row < 67) & inside(c, gx, 32, nx), weight(row - 1 - 2 * c), 0.0).astype(BF16)
     xr2[0:128], xr2[128:256] = high, high
     m_col, m_row, c_col, c_row = col - 1, row - 1, col - 2, row - 2
     up1 = pick(m_row < 66, weight(col - 2 * m_row), 0.0)
@@ -342,7 +344,7 @@
             f0[t, planes] = v[:, 128 * t : 128 * (t + 1)].reshape(16, 48, 128)
         return 0
 
-    lax.fori_loop(0, 3, conv_x0, 0)
+    lax.fori_loop(0, 2, conv_x0, 0)
 
     finish(0)
     receive(1, False)
@@ -359,18 +361,29 @@
     high, low = split(join([r1[p] for p in range(15)], 1))
     v = dot(yr2[:, 0:40], high) + dot(yr2[:, 0:40], low)
     v = dot(join(split(join(pieces(v, 15), 0)), 1), xr2[...]).reshape(15, 24, 128)
+    place = iota((24, 128), 1) // 16
+    for g, offset in enumerate(LEVELS[2]["groups"]):
+        faces = [jnp.zeros((24, 128), F32) for _ in range(2)]
+        for j in range(min(8, 15 - offset)):
+            moved = pltpu.roll(v[offset + j], (16 * j - 48) % 128, 1)
+            faces = [pick(place == (j + f) % 8, moved, faces[f]) for f in range(2)]
+        for f in range(2):
+            pk2[f, g] = faces[f]
+    send(2, True)
+    own = iota((24, 128), 1) < 37
     for g in range(6):
         w = None
         for k in range(3):
             p = 3 * g - 2 + k
             if 0 <= p < 15:
-                part = pltpu.roll(v[p], 42 * k, 1) if k else v[p]
+                part = pick(own, v[p], 0.0)
+                part = pltpu.roll(part, 42 * k, 1) if k else part
                 w = part if w is None else w + part
         e2[3 + g, 8:24, :] = w[0:16]
         e2[3 + g, 32:40, :] = w[16:24]
-    pack_faces(2)
-    send(2, True)
     send(2, False)
+
+    lax.fori_loop(2, 3, conv_x0, 0)
 
     def fine_y(i, _):
         for t in range(2):
@@ -434,10 +447,10 @@
 
     lax.fori_loop(0, 4, add_middle, 0)
 
+    receive(2, False)
+    unpack_own(v2)
     finish(1)
     finish(2)
-    receive(2, False)
-    unpack_own(v2)
     receive(2, True)
     unpack(2, v2)
 

time: 30.6 us -> 30.1 us (0.984)
  Pallas kernels: 29.7 us -> 29.3 us
    pallas_call x1, Pallas kernels: 29.7 us -> 29.3 us  [local(): pl.pallas_call(functools.partial(kernel, counts), out_shape=jax.ShapeDtyp...]
where the time goes in v6:
time: 30.1 us
  Pallas kernels  29.3 us (97%)
  local copies, waits for them, and re-layouts  0.8 us (3%)
    pallas_call x1, Pallas kernels, local(): pl.pallas_call(functools.partial(kernel, counts), out_shape=jax.ShapeDtyp...  29.3 us
    unnamed x1, local copies, waits for them, and re-layouts  0.8 us

profile of v6, /device:TPU:7, one launch (start us, length us, event | category | flops | bytes accessed | tf_op | source)
XLA Modules:
  0.0 30.1 jit_solution(14695660944957816925)
XLA Ops:
  0.0 29.3 %shard_map.28 = f32[16,2,32,128]{3,2,1,0:T(8,128)S(1)} custom-call(f32[32,32,128]{2,1,0:T(8,128)} %q_hbm.1, f32[3,2,17]{2,1,0:T(2,128)} %taps_hbm.1), custom_call_target="tpu_custom_call" | custom-call | tf_op jit(solution)/shard_map/pallas_call | solution.py:508
  29.3 0.8 %copy.4 = f32[32,32,128]{2,1,0:T(8,128)} copy(f32[32,32,128]{2,1,0:T(8,128)S(1)} %bitcast.1) | data formatting | bytes 1048576

commit v7 on v6

--- a/solution.py
+++ b/solution.py
@@ -26,7 +26,7 @@
          py={0: (0, 8, 16), 1: (0, 0, 8), -1: (16, 24, 8)}, pg={0: (0, 1, 2), 1: (0, 0, 1), -1: (2, 3, 1)},
          face=(21, 0), hi=(50, 13, 0), lo=(37, 13, 3), runs=((0, 7, 0, 1), (7, 8, 1, 0), (15, 7, 2, 0), (22, 7, 3, 0))),
 )
-STEPS = tuple((dz, dy, dx) for dx in (1, -1, 0) for dy in (1, -1, 0) for dz in (1, -1, 0) if (dz, dy, dx) != (0, 0, 0))
+STEPS = tuple((dz, dy, dx) for xs in ((1, -1), (0,)) for dy in (1, -1, 0) for dz in (1, -1, 0) for dx in xs if (dz, dy, dx) != (0, 0, 0))
 
 
 def coarse_place(e):

time: 30.1 us -> 30.2 us (level)
  no operation moved by 1% of the time
where the time goes in v7:
time: 30.2 us; the launch traced here: 30.1 us
  Pallas kernels  29.3 us (97%)
  local copies, waits for them, and re-layouts  0.8 us (3%)
    pallas_call x1, Pallas kernels, local(): pl.pallas_call(functools.partial(kernel, counts), out_shape=jax.ShapeDtyp...  29.3 us
    unnamed x1, local copies, waits for them, and re-layouts  0.8 us

profile of v7, /device:TPU:7, one launch (start us, length us, event | category | flops | bytes accessed | tf_op | source)
XLA Modules:
  0.0 30.1 jit_solution(3193270438506802792)
XLA Ops:
  0.0 29.3 %shard_map.28 = f32[16,2,32,128]{3,2,1,0:T(8,128)S(1)} custom-call(f32[32,32,128]{2,1,0:T(8,128)} %q_hbm.1, f32[3,2,17]{2,1,0:T(2,128)} %taps_hbm.1), custom_call_target="tpu_custom_call" | custom-call | tf_op jit(solution)/shard_map/pallas_call | solution.py:508
  29.3 0.8 %copy.4 = f32[32,32,128]{2,1,0:T(8,128)} copy(f32[32,32,128]{2,1,0:T(8,128)S(1)} %bitcast.1) | data formatting | bytes 1048576
